TPU v7x, 32 devices: a whole 2x2x4 slice. The times are simulated.
32 devices in a mesh: groups: 2 (over x), heads: 16 (over z, y, core).
Axes of the slice: x: 2, y: 2, z: 4, core: 2. Of those that a mesh axis runs over, the one named last changes fastest.
Arguments:
- tokens: bfloat16 [64, 4, 2304], P('groups'), parts along dimension 0, may hold values from -6 to 6
- qkv_weight: bfloat16 [4608, 12288], P(('groups', 'heads')), parts along dimension 0, may hold values from -0.125 to 0.125
- gate_weight: bfloat16 [4608, 64], P(('groups', 'heads')), parts along dimension 0, may hold values from -0.125 to 0.125
- conv_weight: bfloat16 [8, 12288], P('groups', 'heads'), parts along dimension 0, may hold values from -3 to 3
- delta_state: float32 [64, 32, 128, 128], P(('groups', 'heads')), parts along dimension 0, may hold values from -0.8 to 0.8
- conv_state: float32 [64, 3, 12288], P(('groups', 'heads')), parts along dimension 0, may hold values from -6 to 6
- old_heads: int32 [32], replicated, may hold values from 0 to 31, each once
- new_units: int32 [64], replicated, may hold values from 0 to 63, each once
- slot_of: int32 [64], P('groups'), parts along dimension 0, may hold values from 0 to 31, each once
- lengths: int32 [64], P('groups'), parts along dimension 0, may hold values from 1 to 4, as said below
Outputs:
- readout: bfloat16 [64, 4, 4096], P('groups', None, 'heads'), parts along dimension 0
There are 2 independent parts, one for each index of `groups`. A program takes and returns all parts, laid end to end along the dimension named above; an argument that names none is the same for every part. Nothing has to cross between parts.
Inputs may be any that keep to these rules, and one draw needn't show every extreme that they name: `old_heads`: a permutation of the heads; old column slot p holds head old_heads[p]. `new_units`: a permutation of the head units; unit u is the half u % 2 of the values of head u // 2. `slot_of`: a permutation of the rows. `lengths`: some row decodes all 4 steps and some row only one.
All inputs are finite; a program needn't handle non-finite values.
Results may differ from a plain program's by a relative error of at most 0.001.
Values may be sent and summed in bfloat16 or wider, within the bound.
A program may use at most 128 MiB of HBM per device.

v0:
```python
import jax
import jax.numpy as jnp
from jax import lax
from jax.sharding import PartitionSpec as P

D = 2304
H = 32
DK = 128
TAPS = 4
STEPS = 4
HALF = 64
UNITS = 64


norm_eps = 1e-06


def unit_tables(old_heads, new_units):
    positions = jnp.arange(H, dtype=jnp.int32)
    inverse = jnp.sum(
        jnp.where(old_heads[None, :] == positions[:, None], positions[None, :], 0), axis=1
    )
    heads_of = new_units // 2
    halves = new_units % 2
    old_slots = jnp.sum(
        jnp.where(heads_of[:, None] == positions[None, :], inverse[None, :], 0), axis=1
    )
    return (old_slots, halves)


def select_units(source, selector, halves, precise):
    lead = source.shape[:-1]
    shaped = source.reshape(lead + (3, H, DK))
    if precise:
        picked = jnp.einsum("...mhk,uh->...muk", shaped, selector, precision=lax.Precision.HIGHEST)
    else:
        picked = jnp.einsum(
            "...mhk,uh->...muk", shaped, selector, preferred_element_type=jnp.float32
        ).astype(source.dtype)
    query_part = picked[..., 0, :, :]
    key_part = picked[..., 1, :, :]
    value_full = picked[..., 2, :, :]
    value_part = jnp.where((halves == 0)[:, None], value_full[..., :HALF], value_full[..., HALF:])
    return jnp.concatenate([query_part, key_part, value_part], axis=-1)


def pick_state(delta_state, selector, halves):
    picked = jnp.einsum("rhkv,uh->rukv", delta_state, selector, precision=lax.Precision.HIGHEST)
    return jnp.where((halves == 0)[None, :, None, None], picked[..., :HALF], picked[..., HALF:])


def normalize(values):
    return values * lax.rsqrt(jnp.sum(values * values, axis=-1, keepdims=True) + norm_eps)


def run_steps(projected, gate_pre, history, tap_weights, carried, live_lengths):
    sequence = jnp.concatenate([history, projected], axis=1)
    weights_f = tap_weights.astype(jnp.float32)
    convolved = weights_f[0][None, None] * sequence[:, 0:STEPS]
    for tap_index in range(1, TAPS):
        convolved = (
            convolved
            + weights_f[tap_index][None, None] * sequence[:, tap_index : tap_index + STEPS]
        )
    activated = jax.nn.silu(convolved)
    queries = normalize(activated[..., :DK])
    keys_all = normalize(activated[..., DK : 2 * DK])
    values_all = activated[..., 2 * DK :]
    beta = jax.nn.sigmoid(gate_pre[..., 0])
    decay = jnp.exp(-jax.nn.softplus(gate_pre[..., 1]))
    readouts = []
    for step_index in range(STEPS):
        is_live = (step_index < live_lengths)[:, None, None, None]
        faded = decay[:, step_index, :, None, None] * carried
        predicted = jnp.sum(keys_all[:, step_index, :, :, None] * faded, axis=2)
        updated = (
            faded
            + beta[:, step_index, :, None, None]
            * keys_all[:, step_index, :, :, None]
            * (values_all[:, step_index] - predicted)[:, :, None, :]
        )
        heads_now = jnp.sum(queries[:, step_index, :, :, None] * updated, axis=2)
        carried = jnp.where(is_live, updated, carried)
        readouts.append(jnp.where(is_live[..., 0], heads_now, jnp.zeros_like(heads_now)))
    return jnp.stack(readouts, axis=1).astype(jnp.bfloat16)


def on_device(
    tokens,
    qkv_weight,
    gate_weight,
    conv_weight,
    delta_state,
    conv_state,
    old_heads,
    new_units,
    slot_of,
    lengths,
):
    devices = lax.axis_size("heads")
    my_index = lax.axis_index("heads")
    per_device = UNITS // devices
    unit_width = 2 * DK + HALF
    old_slots, halves = unit_tables(old_heads, new_units)
    head_range = jnp.arange(H, dtype=jnp.int32)
    selector_bits = old_slots[:, None] == head_range[None, :]
    selector_low = selector_bits.astype(jnp.bfloat16)
    selector_full = selector_bits.astype(jnp.float32)
    local_rows = qkv_weight.shape[0]
    packed = select_units(qkv_weight, selector_low, halves, False).reshape(
        local_rows, devices, per_device, unit_width
    )
    gate_shaped = gate_weight.reshape(local_rows, 2, H)
    packed_gate = jnp.einsum(
        "rmh,uh->rum", gate_shaped, selector_low, preferred_element_type=jnp.float32
    ).astype(jnp.bfloat16)
    packed_gate = packed_gate.reshape(local_rows, devices, per_device, 2)
    mine_weight, mine_gate = (
        lax.all_to_all(packed, "heads", split_axis=1, concat_axis=0, tiled=True),
        lax.all_to_all(packed_gate, "heads", split_axis=1, concat_axis=0, tiled=True),
    )
    row_count = tokens.shape[0]
    row_range = jnp.arange(row_count, dtype=jnp.int32)
    match_rows = slot_of[None, :] == row_range[:, None]
    to_old = match_rows.astype(jnp.bfloat16)
    tokens_old = jnp.einsum(
        "ob,bsd->osd", to_old, tokens, preferred_element_type=jnp.float32
    ).astype(jnp.bfloat16)
    lengths_old = jnp.sum(jnp.where(match_rows, lengths[None, :], 0), axis=1)
    flattened = tokens_old.reshape(row_count * STEPS, D)
    projected = jnp.dot(
        flattened,
        mine_weight.reshape(D, per_device * unit_width),
        preferred_element_type=jnp.float32,
    ).reshape(row_count, STEPS, per_device, unit_width)
    gate_pre = jnp.dot(
        flattened, mine_gate.reshape(D, per_device * 2), preferred_element_type=jnp.float32
    ).reshape(row_count, STEPS, per_device, 2)
    taps_all = lax.all_gather(conv_weight, "heads", axis=1, tiled=True)
    tap_table = select_units(taps_all, selector_low, halves, False)
    rows_dev = delta_state.shape[0]
    got_projected, got_gate = (
        lax.all_to_all(projected, "heads", split_axis=0, concat_axis=2, tiled=True),
        lax.all_to_all(gate_pre, "heads", split_axis=0, concat_axis=2, tiled=True),
    )
    live_lengths = lax.dynamic_slice_in_dim(lengths_old, my_index * rows_dev, rows_dev, 0)
    history = select_units(conv_state, selector_full, halves, True)
    carried = pick_state(delta_state, selector_full, halves)
    local_out = run_steps(got_projected, got_gate, history, tap_table, carried, live_lengths)
    outputs_old = lax.all_to_all(local_out, "heads", split_axis=2, concat_axis=0, tiled=True)
    flat_old = outputs_old.reshape(row_count, STEPS, per_device * HALF)
    outputs = jnp.einsum(
        "ob,osc->bsc", to_old, flat_old, preferred_element_type=jnp.float32
    ).astype(jnp.bfloat16)
    return outputs


def solution(mesh):
    in_specs = (
        P("groups", None, None),
        P(("groups", "heads"), None),
        P(("groups", "heads"), None),
        P("groups", "heads"),
        P(("groups", "heads"), None, None, None),
        P(("groups", "heads"), None, None),
        P(),
        P(),
        P("groups"),
        P("groups"),
    )
    out_specs = P("groups", None, "heads")
    return jax.shard_map(
        on_device, mesh=mesh, in_specs=in_specs, out_specs=out_specs, check_vma=False
    )
```

profile of v0, /device:TPU:0, one launch (start us, length us, event | category | flops | bytes accessed | tf_op | source)
XLA Modules:
  0.0 336.9 jit_solution(10728899009877708103)
XLA Ops:
  1.6 1.0 fusion.9
  3.2 7.4 %all-to-all-start.2 = ((bf16[144,16,4,2]{0,3,2,1:T(2,128)(2,1)}), bf16[144,16,4,2]{0,3,2,1:T(2,128)(2,1)S(1)}, u32[]{:S(2)}, u32[]{:S(2)}) async-start(bf16[144,16,4,2]{0,3,2,1:T(2,128)(2,1)} %bitcast.40), calls=%async_computation.2 | async-start | bytes 131072 | tf_op jit(solution)/shard_map/all_to_all | solution.py:120
  11.3 2.7 copy.172
  14.1 2.0 convert_bitcast_fusion
  16.1 2.5 fusion.52
  19.4 6.9 %pad_maximum_fusion = bf16[144,16,4,320]{3,2,1,0:T(4,128)(2,1)} fusion(bf16[144,16,4,64]{3,2,1,0:T(4,128)(2,1)S(1)} %bitcast.162, bf16[144,16,4,128]{3,2,1,0:T(4,128)(2,1)S(1)} %bitcast.161, bf16[144,16,4,128]{3,2,1,0:T(4,128)(2,1)S(1)} %bitcast.160), kind=kLoop, calls=%fused_computation.15 | loop fusion | flops 17694720 | bytes 11796480 | tf_op jit(solution)/shard_map/concatenate | solution.py:44
  26.3 9.1 %copy.167 = bf16[144,16,4,320]{3,2,0,1:T(4,128)(2,1)} copy(bf16[144,16,4,320]{3,2,1,0:T(4,128)(2,1)} %pad_maximum_fusion) | data formatting | bytes 11796480 | tf_op jit(solution)/shard_map/concatenate | solution.py:44
  35.4 6.2 %all-to-all-start = ((bf16[144,16,4,320]{3,2,0,1:T(4,128)(2,1)}), bf16[144,16,4,320]{3,2,0,1:T(4,128)(2,1)}, u32[]{:S(2)}, u32[]{:S(2)}) async-start(bf16[144,16,4,320]{3,2,0,1:T(4,128)(2,1)} %copy.167), calls=%async_computation | async-start | bytes 14155776 | tf_op jit(solution)/shard_map/all_to_all | solution.py:119
  41.6 141.3 %all_gather.3 = bf16[4,12288]{1,0:T(4,128)(2,1)S(1)} all-gather(bf16[4,768]{1,0:T(4,128)(2,1)S(1)} %copy-done.3), channel_id=1, replica_groups=mesh['groups'=2,'heads'=16] {'heads'}, dimensions={1}, use_global_device_ids=true | all-gather | bytes 104448 | tf_op jit(solution)/shard_map/all_gather | solution.py:139
  185.4 11.6 %fusion.5 = f32[2,64,128,128]{3,1,2,0:T(8,128)} fusion(f32[2,32,128,128]{3,2,1,0:T(8,128)} %param.14, s32[64]{0:T(128)S(1)} %select_reduce_fusion), kind=kOutput, calls=%fused_computation.21 | convolution fusion | flops 805308416 | bytes 12583168 | tf_op jit(solution)/shard_map/rhkv,uh->rukv/dot_general | solution.py:48
  198.5 27.5 %all-to-all-start.3 = ((f32[32,4,4,2]{2,3,1,0:T(2,128)}), f32[32,4,4,2]{2,3,1,0:T(2,128)S(1)}, u32[]{:S(2)}, u32[]{:S(2)}) async-start(f32[32,4,4,2]{2,3,1,0:T(2,128)} %copy.143), calls=%async_computation.3 | async-start | bytes 262144 | tf_op jit(solution)/shard_map/all_to_all | solution.py:144
  226.0 11.9 %reshape.189 = bf16[2304,1280]{1,0:T(8,128)(2,1)} reshape(bf16[16,144,1,4,320]{4,3,1,0,2:T(4,128)(2,1)} %bitcast.24) | data formatting | bytes 11796480 | tf_op jit(solution)/shard_map/reshape | solution.py:133
  237.8 8.9 %copy.135 = bf16[1280,2304]{1,0:T(8,128)(2,1)} copy(bf16[1280,2304]{0,1:T(8,128)(2,1)} %bitcast.158) | data formatting | bytes 11796480 | tf_op jit(solution)/shard_map/dot_general | solution.py:131
  246.7 4.7 %fusion.58 = f32[32,4,4,320]{3,0,2,1:T(8,128)S(1)} fusion(bf16[32,4,2304,1]{2,0,3,1:T(8,128)(2,1)S(1)} %fusion.4, bf16[4,320,2304,1]{2,1,0,3:T(8,128)(2,1)} %bitcast.163), kind=kOutput, calls=%fused_computation.124 | convolution fusion | flops 754974720 | bytes 7143424 | tf_op jit(solution)/shard_map/dot_general | solution.py:131
  251.5 1.4 copy.136
  252.9 6.0 %all-to-all-start.1 = ((f32[32,4,4,320]{3,2,1,0:T(4,128)}), f32[32,4,4,320]{3,2,1,0:T(4,128)S(1)}, u32[]{:S(2)}, u32[]{:S(2)}) async-start(f32[32,4,4,320]{3,2,1,0:T(4,128)} %copy.136), calls=%async_computation.1 | async-start | bytes 1572864 | tf_op jit(solution)/shard_map/all_to_all | solution.py:143
  259.3 18.3 %all-to-all-done.1 = f32[32,4,4,320]{3,2,1,0:T(4,128)S(1)} async-done(((f32[32,4,4,320]{3,2,1,0:T(4,128)}), f32[32,4,4,320]{3,2,1,0:T(4,128)S(1)}, u32[]{:S(2)}, u32[]{:S(2)}) %all-to-all-start.1) | async-done | bytes 655392 | tf_op jit(solution)/shard_map/all_to_all | solution.py:143
  277.8 1.5 divide_multiply_fusion
  282.2 8.5 %multiply_reduce_fusion.7 = (f32[2,64,64]{2,1,0:T(8,128)S(1)}, f32[2,64,128,64]{3,1,2,0:T(8,128)S(1)}) fusion(f32[2,64,128]{1,2,0:T(8,128)S(1)} %copy.148, f32[2,64]{1,0:T(2,128)S(1)} %bitcast.195, f32[2,64,128,128]{3,1,2,0:T(8,128)} %fusion.5, pred[64]{0:T(512)(128)(4,1)S(1)} %fusion.50), kind=kLoop, calls=%fused_computation.12 | loop fusion | flops 4186112 | bytes 12681792 | tf_op jit(solution)/shard_map/reduce_sum | solution.py:75
  290.7 5.1 %multiply_reduce_fusion.5 = f32[2,64,64]{2,1,0:T(8,128)S(1)} fusion(f32[2,64,128,64]{3,1,2,0:T(8,128)S(1)} %get-tuple-element.16, f32[2,64,128]{1,2,0:T(8,128)S(1)} %copy.151, f32[2,64]{1,0:T(2,128)S(1)} %bitcast.202, f32[2,64,64]{2,1,0:T(8,128)S(1)} %sub.35, f32[2,64,128]{1,2,0:T(8,128)S(1)} %copy.147, f32[2,64]{1,0:T(2,128)S(1)} %bitcast.196, ...), kind=kLoop, calls=%fused_computation.9 | loop fusion | flops 7331840 | bytes 4391938 | tf_op jit(solution)/shard_map/reduce_sum | solution.py:75
  295.8 11.4 %multiply_reduce_fusion.6 = (bf16[2,64,64]{2,1,0:T(8,128)(2,1)S(1)}, bf16[2,64,64]{2,1,0:T(8,128)(2,1)S(1)}, f32[2,64,64]{2,1,0:T(8,128)S(1)}, f32[2,64,128,64]{3,1,2,0:T(8,128)S(1)}) fusion(f32[2,64,128,64]{3,1,2,0:T(8,128)S(1)} %get-tuple-element.16, f32[2,64,64]{2,1,0:T(8,128)S(1)} %sub.35, f32[2,64,128]{1,2,0:T(8,128)S(1)} %copy.147, ...), kind=kLoop, calls=%fused_computation.10 | loop fusion | flops 15704064 | bytes 8848900 | tf_op jit(solution)/shard_map/reduce_sum | solution.py:82
  307.3 5.1 %multiply_reduce_fusion.1 = f32[2,64,64]{2,1,0:T(8,128)S(1)} fusion(f32[2,64,128,64]{3,1,2,0:T(8,128)S(1)} %get-tuple-element.18, f32[2,64,128]{1,2,0:T(8,128)S(1)} %copy.157, f32[2,64]{1,0:T(2,128)S(1)} %bitcast.200, f32[2,64,64]{2,1,0:T(8,128)S(1)} %sub.37, f32[2,64,128]{1,2,0:T(8,128)S(1)} %copy.153, f32[2,64]{1,0:T(2,128)S(1)} %bitcast.193, ...), kind=kLoop, calls=%fused_computation.2 | loop fusion | flops 7331840 | bytes 4391938 | tf_op jit(solution)/shard_map/reduce_sum | solution.py:75
  312.4 10.5 %multiply_reduce_fusion.2 = (bf16[2,64,64]{2,1,0:T(8,128)(2,1)S(1)}, bf16[2,64,64]{2,1,0:T(8,128)(2,1)S(1)}) fusion(f32[2,64,128,64]{3,1,2,0:T(8,128)S(1)} %get-tuple-element.18, f32[2,64,64]{2,1,0:T(8,128)S(1)} %sub.37, f32[2,64,128]{1,2,0:T(8,128)S(1)} %copy.153, f32[2,64]{1,0:T(2,128)S(1)} %bitcast.194, f32[2,64,128]{1,2,0:T(8,128)S(1)} %copy.152, ...), kind=kLoop, calls=%fused_computation.4 | loop fusion | flops 11517952 | bytes 4555778 | tf_op jit(solution)/shard_map/reduce_sum | solution.py:82
  323.6 12.1 %all_to_all.81 = bf16[16,2,1024]{2,1,0:T(2,128)(2,1)S(1)} all-to-all(bf16[16,2,1024]{2,1,0:T(2,128)(2,1)S(1)} %reshape.202), channel_id=1, replica_groups=mesh['groups'=2,'heads'=16] {'heads'}, dimensions={0} | all-to-all | bytes 131072 | tf_op jit(solution)/shard_map/all_to_all | solution.py:150
  (89 shorter events, 12.6 us)
Async XLA Ops:
  0.0 184.6 %copy-start = (bf16[32,4,2304]{2,1,0:T(4,128)(2,1)S(1)}, bf16[32,4,2304]{2,1,0:T(4,128)(2,1)}, u32[]{:S(2)}) copy-start(bf16[32,4,2304]{2,1,0:T(4,128)(2,1)} %param.10) | copy-start | bytes 1769476
  3.2 32.2 %all-to-all-start.2 = ((bf16[144,16,4,2]{0,3,2,1:T(2,128)(2,1)}), bf16[144,16,4,2]{0,3,2,1:T(2,128)(2,1)S(1)}, u32[]{:S(2)}, u32[]{:S(2)}) async-start(bf16[144,16,4,2]{0,3,2,1:T(2,128)(2,1)} %bitcast.40), calls=%async_computation.2 | async-start | bytes 131072 | tf_op jit(solution)/shard_map/all_to_all | solution.py:120
  35.4 6.2 %copy-start.3 = (bf16[4,768]{1,0:T(4,128)(2,1)S(1)}, bf16[4,768]{1,0:T(4,128)(2,1)}, u32[]{:S(2)}) copy-start(bf16[4,768]{1,0:T(4,128)(2,1)} %param.13) | copy-start | bytes 18436
  35.4 147.6 %copy-start.2 = (f32[2,3,12288]{2,0,1:T(2,128)S(1)}, f32[2,3,12288]{2,0,1:T(2,128)}, u32[]{:S(2)}) copy-start(f32[2,3,12288]{2,0,1:T(2,128)} %param.15) | copy-start | bytes 884740
  35.4 149.0 %copy-start.4 = (s32[32]{0:T(128)S(1)}, s32[32]{0:T(128)}, u32[]{:S(2)}) copy-start(s32[32]{0:T(128)} %param.18) | copy-start | bytes 388
  35.4 149.0 %copy-start.5 = (s32[32]{0:T(128)S(1)}, s32[32]{0:T(128)}, u32[]{:S(2)}) copy-start(s32[32]{0:T(128)} %param.19) | copy-start | bytes 388
  35.4 163.0 %all-to-all-start = ((bf16[144,16,4,320]{3,2,0,1:T(4,128)(2,1)}), bf16[144,16,4,320]{3,2,0,1:T(4,128)(2,1)}, u32[]{:S(2)}, u32[]{:S(2)}) async-start(bf16[144,16,4,320]{3,2,0,1:T(4,128)(2,1)} %copy.167), calls=%async_computation | async-start | bytes 14155776 | tf_op jit(solution)/shard_map/all_to_all | solution.py:119
  198.5 54.4 %all-to-all-start.3 = ((f32[32,4,4,2]{2,3,1,0:T(2,128)}), f32[32,4,4,2]{2,3,1,0:T(2,128)S(1)}, u32[]{:S(2)}, u32[]{:S(2)}) async-start(f32[32,4,4,2]{2,3,1,0:T(2,128)} %copy.143), calls=%async_computation.3 | async-start | bytes 262144 | tf_op jit(solution)/shard_map/all_to_all | solution.py:144
  252.9 24.7 %all-to-all-start.1 = ((f32[32,4,4,320]{3,2,1,0:T(4,128)}), f32[32,4,4,320]{3,2,1,0:T(4,128)S(1)}, u32[]{:S(2)}, u32[]{:S(2)}) async-start(f32[32,4,4,320]{3,2,1,0:T(4,128)} %copy.136), calls=%async_computation.1 | async-start | bytes 1572864 | tf_op jit(solution)/shard_map/all_to_all | solution.py:143
  307.3 29.6 %copy-start.1 = (bf16[32,4,2304]{2,1,0:T(4,128)(2,1)S(1)}, bf16[32,4,2304]{2,1,0:T(4,128)(2,1)}, u32[]{:S(2)}) copy-start(bf16[32,4,2304]{2,1,0:T(4,128)(2,1)} %param.10) | copy-start | bytes 1769476
where the time goes:
time: 338 us; the launch traced here: 337 us
  blocking collectives  153 us (45%)
  other arithmetic  54 us (16%)
  starting transfers between devices  47.1 us (14%)
  local copies, waits for them, and re-layouts  42.4 us (13%)
  matrix products  21.1 us (6%)
  waiting for transfers between devices  18.3 us (5%)
    all_gather x1, blocking collectives, on_device(): taps_all = lax.all_gather(conv_weight, 'heads', axis=1, tiled=True)  141 us
    all_to_all x1, starting transfers between devices, on_device(): lax.all_to_all(gate_pre, 'heads', split_axis=0, concat_axis=2, tiled=True)  27.5 us
    reduce_sum x2, other arithmetic, run_steps(): heads_now = jnp.sum(queries[:, step_index, :, :, None] * updated, axis=2)  22 us
    reduce_sum x3, other arithmetic, run_steps(): predicted = jnp.sum(keys_all[:, step_index, :, :, None] * faded, axis=2)  18.7 us
    all_to_all x1, waiting for transfers between devices, on_device(): lax.all_to_all(projected, 'heads', split_axis=0, concat_axis=2, tiled=True)  18.3 us
    all_to_all x1, blocking collectives, on_device(): lax.all_to_all(local_out, 'heads', split_axis=2, concat_axis=0, tiled=True)  12.1 us
    reshape x1, local copies, waits for them, and re-layouts, on_device(): mine_weight.reshape(D, per_device * unit_width)  11.9 us
    dot_general x1, matrix products, pick_state(): jnp.einsum('rhkv,uh->rukv', delta_state, selector, precision=lax.Precisio...  11.6 us
  transfers between devices with their start and end apart: 4, of which 1 were waited for; matrix products, arithmetic and copies ran while one was open for 20% of the time, Pallas kernels for 0%

commit v1 on v0

v1 whole, which is shorter than its diff:
```python
import jax
import jax.numpy as jnp
from jax import lax
from jax.sharding import PartitionSpec as P

H = 32
DK = 128
TAPS = 4
STEPS = 4
HALF = 64
UNITS = 64
CHANNELS = 3 * H * DK

norm_eps = 1e-06


def unit_positions(old_heads, new_units):
    positions = jnp.arange(H, dtype=jnp.int32)
    inverse = jnp.sum(
        jnp.where(old_heads[None, :] == positions[:, None], positions[None, :], 0), axis=1
    )
    heads_of = new_units // 2
    old_slots = jnp.sum(
        jnp.where(heads_of[:, None] == positions[None, :], inverse[None, :], 0), axis=1
    )
    return old_slots * 2 + new_units % 2


def normalize(values):
    return values * lax.rsqrt(jnp.sum(values * values, axis=-1, keepdims=True) + norm_eps)


def decode(projected, gate_pre, history, taps, state, live_lengths):
    rows = projected.shape[0]
    sequence = jnp.concatenate([history, projected], axis=1)
    weights_f = taps.astype(jnp.float32)
    convolved = weights_f[0][None, None] * sequence[:, 0:STEPS]
    for tap_index in range(1, TAPS):
        convolved = (
            convolved
            + weights_f[tap_index][None, None] * sequence[:, tap_index : tap_index + STEPS]
        )
    activated = jax.nn.silu(convolved).reshape(rows, STEPS, 3, H, DK)
    queries = normalize(activated[:, :, 0])
    keys = normalize(activated[:, :, 1])
    values = activated[:, :, 2]
    beta = jax.nn.sigmoid(gate_pre[:, :, 0])
    decay = jnp.exp(-jax.nn.softplus(gate_pre[:, :, 1]))
    both = jnp.concatenate([queries, keys], axis=1)
    based = jnp.einsum("rihk,rhkv->rihv", both, state, precision=lax.Precision.HIGHEST)
    query_base, key_base = based[:, :STEPS], based[:, STEPS:]

    corrections = []
    outs = []
    faded_base = jnp.ones_like(decay[:, 0])
    spans = []
    for s in range(STEPS):
        faded_base = faded_base * decay[:, s]
        spans = [span * decay[:, s] for span in spans]
        predicted = faded_base[..., None] * key_base[:, s]
        for j in range(s):
            overlap = jnp.sum(keys[:, s] * keys[:, j], axis=-1) * spans[j]
            predicted = predicted + overlap[..., None] * corrections[j]
        corrections.append(beta[:, s, :, None] * (values[:, s] - predicted))
        spans.append(jnp.ones_like(faded_base))
        now = faded_base[..., None] * query_base[:, s]
        for j in range(s + 1):
            overlap = jnp.sum(queries[:, s] * keys[:, j], axis=-1) * spans[j]
            now = now + overlap[..., None] * corrections[j]
        live = (s < live_lengths)[:, None, None]
        outs.append(jnp.where(live, now, jnp.zeros_like(now)))
    return jnp.stack(outs, axis=1).astype(jnp.bfloat16)


def on_device(
    tokens,
    qkv_weight,
    gate_weight,
    conv_weight,
    delta_state,
    conv_state,
    old_heads,
    new_units,
    slot_of,
    lengths,
):
    devices = lax.axis_size("heads")
    my_index = lax.axis_index("heads")
    row_count = tokens.shape[0]
    rows_dev = delta_state.shape[0]
    depth = qkv_weight.shape[0]
    taps = lax.all_gather(conv_weight, "heads", axis=1, tiled=True)

    row_range = jnp.arange(row_count, dtype=jnp.int32)
    to_old = (slot_of[None, :] == row_range[:, None]).astype(jnp.bfloat16)
    tokens_old = jnp.einsum(
        "ob,bsd->osd", to_old, tokens, preferred_element_type=jnp.float32
    ).astype(jnp.bfloat16)
    width = tokens.shape[2]
    columns = H * DK // devices
    shaped = qkv_weight.reshape(depth, 3, devices, columns)
    mine_weight = lax.all_to_all(shaped, "heads", split_axis=2, concat_axis=0, tiled=True)
    projected_all = jnp.dot(
        tokens_old.reshape(row_count * STEPS, width),
        mine_weight.reshape(width, 3 * columns),
        preferred_element_type=jnp.float32,
    ).reshape(row_count, STEPS, 3, 1, columns)
    projected = lax.all_to_all(
        projected_all, "heads", split_axis=0, concat_axis=3, tiled=True
    ).reshape(rows_dev, STEPS, CHANNELS)
    gates_all = lax.all_gather(gate_weight, "heads", axis=0, tiled=True)
    my_tokens = lax.dynamic_slice_in_dim(tokens_old, my_index * rows_dev, rows_dev, 0)
    gate_pre = jnp.dot(
        my_tokens.reshape(rows_dev * STEPS, width), gates_all, preferred_element_type=jnp.float32
    ).reshape(rows_dev, STEPS, 2, H)

    my_slots = my_index * rows_dev + jnp.arange(rows_dev, dtype=jnp.int32)
    live_lengths = jnp.sum(
        jnp.where(slot_of[None, :] == my_slots[:, None], lengths[None, :], 0), axis=1
    )
    heads_out = decode(projected, gate_pre, conv_state, taps, delta_state, live_lengths)

    unit_from = unit_positions(old_heads, new_units)
    pick = (unit_from[:, None] == jnp.arange(UNITS, dtype=jnp.int32)[None, :]).astype(jnp.bfloat16)
    units_out = jnp.einsum(
        "rsxc,ux->rsuc",
        heads_out.reshape(rows_dev, STEPS, UNITS, HALF),
        pick,
        preferred_element_type=jnp.float32,
    ).astype(jnp.bfloat16)
    outputs_old = lax.all_to_all(units_out, "heads", split_axis=2, concat_axis=0, tiled=True)
    flat_old = outputs_old.reshape(row_count, STEPS, (UNITS // devices) * HALF)
    return jnp.einsum(
        "ob,osc->bsc", to_old, flat_old, preferred_element_type=jnp.float32
    ).astype(jnp.bfloat16)


def solution(mesh):
    in_specs = (
        P("groups", None, None),
        P(("groups", "heads"), None),
        P(("groups", "heads"), None),
        P("groups", "heads"),
        P(("groups", "heads"), None, None, None),
        P(("groups", "heads"), None, None),
        P(),
        P(),
        P("groups"),
        P("groups"),
    )
    return jax.shard_map(
        on_device,
        mesh=mesh,
        in_specs=in_specs,
        out_specs=P("groups", None, "heads"),
        check_vma=False,
    )
```

time: 338 us -> 184 us (0.54)
  other arithmetic: 54 us -> 6.35 us
  starting transfers between devices: 47.1 us -> 11.3 us
  blocking collectives: 153 us -> 120 us
  local copies, waits for them, and re-layouts: 42.4 us -> 23.8 us
  matrix products: 21.1 us -> 9.83 us
  waiting for transfers between devices: 18.3 us -> 11.7 us
    reduce_sum x8 -> x4, other arithmetic: 41.6 us -> 2.61 us  [the longest x1 2.23 us: decode(): overlap = jnp.sum(queries[:, s] * keys[:, j], axis=-1) * spans[j]]
    all_to_all x4 -> x2, starting transfers between devices: 47.1 us -> 11.3 us  [the longest x1 7.6 us: on_device(): lax.all_to_all(shaped, 'heads', split_axis=2, concat_axis=0, tiled=True)]
    all_gather x1 -> x2, blocking collectives: 141 us -> 110 us  [the longest x1 76.9 us: on_device(): gates_all = lax.all_gather(gate_weight, 'heads', axis=0, tiled=True)]
    dot_general x7 -> x4, matrix products: 20.5 us -> 9.19 us  [the longest x1 5.3 us: decode(): jnp.einsum('rihk,rhkv->rihv', both, state, precision=lax.Precision.HIGHEST)]
    concatenate x2 -> x0, local copies, waits for them, and re-layouts: 9.54 us -> none  [select_units(): return jnp.concatenate([query_part, key_part, value_part], axis=-1)]
    reshape x5 -> x4, local copies, waits for them, and re-layouts: 13.1 us -> 3.76 us  [the longest x1 3.14 us: on_device(): shaped = qkv_weight.reshape(depth, 3, devices, columns)]
    concatenate x2 -> x0, other arithmetic: 6.96 us -> none  [select_units(): return jnp.concatenate([query_part, key_part, value_part], axis=-1)]
    all_to_all x4 -> x2, waiting for transfers between devices: 18.3 us -> 11.7 us  [the longest x1 11.6 us: on_device(): lax.all_to_all(projected_all, 'heads', split_axis=0, concat_axis=3, tiled...]
  transfers between devices with their start and end apart: 4 -> 2, of which waited for: 1 -> 1; matrix products, arithmetic and copies ran while one was open for 20% -> 1% of each run, Pallas kernels for 0% -> 0%
where the time goes in v1:
time: 184 us
  blocking collectives  120 us (65%)
  local copies, waits for them, and re-layouts  23.8 us (13%)
  waiting for transfers between devices  11.7 us (6%)
  starting transfers between devices  11.3 us (6%)
  matrix products  9.83 us (5%)
  other arithmetic  6.35 us (3%)
    all_gather x1, blocking collectives, on_device(): gates_all = lax.all_gather(gate_weight, 'heads', axis=0, tiled=True)  76.9 us
    all_gather x1, blocking collectives, on_device(): taps = lax.all_gather(conv_weight, 'heads', axis=1, tiled=True)  33.4 us
    all_to_all x1, waiting for transfers between devices, on_device(): lax.all_to_all(projected_all, 'heads', split_axis=0, concat_axis=3, tiled...  11.6 us
    all_to_all x1, blocking collectives, on_device(): lax.all_to_all(units_out, 'heads', split_axis=2, concat_axis=0, tiled=True)  10.1 us
    all_to_all x1, starting transfers between devices, on_device(): lax.all_to_all(shaped, 'heads', split_axis=2, concat_axis=0, tiled=True)  7.6 us
    unnamed x23, local copies, waits for them, and re-layouts  7.01 us
    dot_general x2, local copies, waits for them, and re-layouts, on_device(): jnp.dot(tokens_old.reshape(row_count * STEPS, width), mine_weight.reshape...  6.78 us
    dot_general x1, matrix products, decode(): jnp.einsum('rihk,rhkv->rihv', both, state, precision=lax.Precision.HIGHEST)  5.3 us
  transfers between devices with their start and end apart: 2, of which 1 were waited for; matrix products, arithmetic and copies ran while one was open for 1% of the time, Pallas kernels for 0%

profile of v1, /device:TPU:0, one launch (start us, length us, event | category | flops | bytes accessed | tf_op | source)
XLA Modules:
  0.0 183.7 jit_solution(12489210930867684894)
XLA Ops:
  0.0 3.0 %copy.122 = bf16[18,8,48,256]{3,2,1,0:T(8,128)(2,1)S(1)} copy(bf16[18,8,48,256]{3,1,2,0:T(8,128)(2,1)} %bitcast.160) | data formatting | bytes 7077888
  3.0 3.1 %copy.98 = bf16[144,3,16,256]{3,0,1,2:T(8,128)(2,1)} copy(bf16[144,3,16,256]{3,2,1,0:T(8,128)(2,1)S(1)} %bitcast.158) | data formatting | bytes 7077888 | tf_op jit(solution)/shard_map/reshape | solution.py:101
  6.2 7.6 %all-to-all-start = ((bf16[144,3,16,256]{3,0,1,2:T(8,128)(2,1)}), bf16[144,3,16,256]{3,0,1,2:T(8,128)(2,1)}, u32[]{:S(2)}, u32[]{:S(2)}) async-start(bf16[144,3,16,256]{3,0,1,2:T(8,128)(2,1)} %copy.98), calls=%async_computation | async-start | bytes 7077888 | tf_op jit(solution)/shard_map/all_to_all | solution.py:102
  13.8 76.9 %all-gather = bf16[16,144,64]{1,2,0:T(8,128)(2,1)S(1)} all-gather(bf16[1,144,64]{1,2,0:T(8,128)(2,1)S(1)} %bitcast.175), channel_id=1, replica_groups=mesh['groups'=2,'heads'=16] {'heads'}, dimensions={0}, use_global_device_ids=true | all-gather | bytes 313344 | tf_op jit(solution)/shard_map/all_gather | solution.py:111
  90.7 0.3 copy.97
  91.0 0.6 reshape.262
  91.6 33.4 %all_gather.7 = bf16[4,12288]{1,0:T(4,128)(2,1)S(1)} all-gather(bf16[4,768]{1,0:T(4,128)(2,1)S(1)} %copy-done.3), channel_id=1, replica_groups=mesh['groups'=2,'heads'=16] {'heads'}, dimensions={1}, use_global_device_ids=true | all-gather | bytes 104448 | tf_op jit(solution)/shard_map/all_gather | solution.py:92
  125.5 0.4 convolution_convert_fusion
  125.9 0.3 fusion.23
  126.4 4.4 %copy.99 = bf16[16,144,3,1,256]{4,2,1,0,3:T(4,128)(2,1)S(1)} copy(bf16[16,144,3,1,256]{4,1,2,0,3:T(8,128)(2,1)} %bitcast.16) | data formatting | bytes 7077888 | tf_op jit(solution)/shard_map/all_to_all | solution.py:102
  130.9 2.8 %copy.123 = bf16[288,8,3,256]{3,1,2,0:T(8,128)(2,1)} copy(bf16[288,8,3,256]{3,2,1,0:T(4,128)(2,1)S(1)} %bitcast.157) | data formatting | bytes 7077888
  133.7 5.8 %copy.100 = bf16[768,2304]{1,0:T(8,128)(2,1)} copy(bf16[768,2304]{0,1:T(8,128)(2,1)} %bitcast.159) | data formatting | bytes 7077888 | tf_op jit(solution)/shard_map/dot_general | solution.py:103
  139.4 3.3 %convolution_bitcast_fusion = f32[32,4,3,1,256]{4,0,2,1,3:T(8,128)S(1)} fusion(bf16[3,256,2304,1]{2,1,0,3:T(8,128)(2,1)} %bitcast.161, bf16[32,4,2304]{2,0,1:T(8,128)(2,1)S(1)} %convolution_convert_fusion), kind=kOutput, calls=%fused_computation.1 | convolution fusion | flops 452984832 | bytes 4521984 | tf_op jit(solution)/shard_map/dot_general | solution.py:103
  142.8 1.0 copy.101
  143.8 3.7 %all-to-all-start.1 = ((f32[32,4,3,1,256]{4,1,3,2,0:T(4,128)}), f32[32,4,3,1,256]{4,1,3,2,0:T(4,128)S(1)}, u32[]{:S(2)}, u32[]{:S(2)}) async-start(f32[32,4,3,1,256]{4,1,3,2,0:T(4,128)} %copy.101), calls=%async_computation.1 | async-start | bytes 786432 | tf_op jit(solution)/shard_map/all_to_all | solution.py:108
  147.8 11.6 %all-to-all-done.1 = f32[32,4,3,1,256]{4,1,3,2,0:T(4,128)S(1)} async-done(((f32[32,4,3,1,256]{4,1,3,2,0:T(4,128)}), f32[32,4,3,1,256]{4,1,3,2,0:T(4,128)S(1)}, u32[]{:S(2)}, u32[]{:S(2)}) %all-to-all-start.1) | async-done | bytes 393248 | tf_op jit(solution)/shard_map/all_to_all | solution.py:108
  159.8 0.7 divide_multiply_fusion
  161.4 2.2 %multiply_reduce_fusion.16 = (f32[2,32]{1,0:T(2,128)S(1)}, f32[2,32]{1,0:T(2,128)S(1)}, f32[2,32]{1,0:T(2,128)S(1)}, f32[2,32]{1,0:T(2,128)S(1)}, f32[2,32]{1,0:...) fusion(f32[2,4,32,128]{3,1,2,0:T(4,128)S(1)} %fusion.21, ...), kind=kLoop, calls=%fused_computation.92 | loop fusion | flops 261120 | bytes 266240 | tf_op jit(solution)/shard_map/reduce_sum | solution.py:68
  163.6 5.3 %convolution_bitcast_fusion.1 = f32[2,8,32,128]{3,1,2,0:T(8,128)S(1)} fusion(f32[2,32,128,128]{3,2,1,0:T(8,128)} %param.14, f32[2,4,32,128]{3,1,2,0:T(4,128)S(1)} %fusion.22, f32[2,4,32,128]{3,1,2,0:T(4,128)S(1)} %fusion.21), kind=kOutput, calls=%fused_computation.2 | convolution fusion | flops 100728832 | bytes 4718592 | tf_op jit(solution)/shard_map/rihk,rhkv->rihv/dot_general | solution.py:50
  169.0 0.3 convert_reduce_fusion.3
  169.4 1.0 convert_reduce_fusion.2
  170.4 1.1 convert_reduce_fusion
  172.3 10.1 %all_to_all.45 = bf16[16,2,1024]{2,1,0:T(2,128)(2,1)S(1)} all-to-all(bf16[16,2,1024]{2,1,0:T(2,128)(2,1)S(1)} %reshape.274), channel_id=1, replica_groups=mesh['groups'=2,'heads'=16] {'heads'}, dimensions={0} | all-to-all | bytes 131072 | tf_op jit(solution)/shard_map/all_to_all | solution.py:131
  183.0 0.7 copy.113
  (53 shorter events, 3.5 us)
Async XLA Ops:
  0.0 125.5 %copy-start = (bf16[32,4,2304]{2,1,0:T(4,128)(2,1)S(1)}, bf16[32,4,2304]{2,1,0:T(4,128)(2,1)}, u32[]{:S(2)}) copy-start(bf16[32,4,2304]{2,1,0:T(4,128)(2,1)} %param.10) | copy-start | bytes 1769476
  6.2 7.7 %copy-start.2 = (bf16[144,64]{0,1:T(8,128)(2,1)S(1)}, bf16[144,64]{0,1:T(8,128)(2,1)}, u32[]{:S(2)}) copy-start(bf16[144,64]{0,1:T(8,128)(2,1)} %param.12) | copy-start | bytes 55300
  6.2 85.5 %copy-start.3 = (bf16[4,768]{1,0:T(4,128)(2,1)S(1)}, bf16[4,768]{1,0:T(4,128)(2,1)}, u32[]{:S(2)}) copy-start(bf16[4,768]{1,0:T(4,128)(2,1)} %param.13) | copy-start | bytes 18436
  6.2 118.9 %copy-start.6 = (s32[32]{0:T(128)S(1)}, s32[32]{0:T(128)}, u32[]{:S(2)}) copy-start(s32[32]{0:T(128)} %param.16) | copy-start | bytes 388
  6.2 119.0 %copy-start.7 = (s32[64]{0:T(128)S(1)}, s32[64]{0:T(128)}, u32[]{:S(2)}) copy-start(s32[64]{0:T(128)} %param.17) | copy-start | bytes 772
  6.2 119.1 %copy-start.4 = (s32[32]{0:T(128)S(1)}, s32[32]{0:T(128)}, u32[]{:S(2)}) copy-start(s32[32]{0:T(128)} %param.18) | copy-start | bytes 388
  6.2 119.1 %copy-start.5 = (s32[32]{0:T(128)S(1)}, s32[32]{0:T(128)}, u32[]{:S(2)}) copy-start(s32[32]{0:T(128)} %param.19) | copy-start | bytes 388
  6.2 120.2 %all-to-all-start = ((bf16[144,3,16,256]{3,0,1,2:T(8,128)(2,1)}), bf16[144,3,16,256]{3,0,1,2:T(8,128)(2,1)}, u32[]{:S(2)}, u32[]{:S(2)}) async-start(bf16[144,3,16,256]{3,0,1,2:T(8,128)(2,1)} %copy.98), calls=%async_computation | async-start | bytes 7077888 | tf_op jit(solution)/shard_map/all_to_all | solution.py:102
  139.4 8.1 %copy-start.1 = (f32[2,3,12288]{2,0,1:T(2,128)S(1)}, f32[2,3,12288]{2,0,1:T(2,128)}, u32[]{:S(2)}) copy-start(f32[2,3,12288]{2,0,1:T(2,128)} %param.15) | copy-start | bytes 884740
  143.8 15.7 %all-to-all-start.1 = ((f32[32,4,3,1,256]{4,1,3,2,0:T(4,128)}), f32[32,4,3,1,256]{4,1,3,2,0:T(4,128)S(1)}, u32[]{:S(2)}, u32[]{:S(2)}) async-start(f32[32,4,3,1,256]{4,1,3,2,0:T(4,128)} %copy.101), calls=%async_computation.1 | async-start | bytes 786432 | tf_op jit(solution)/shard_map/all_to_all | solution.py:108

commit v2 on v1

--- a/solution.py
+++ b/solution.py
@@ -1,6 +1,10 @@
+import functools
+
 import jax
 import jax.numpy as jnp
 from jax import lax
+from jax.experimental import pallas as pl
+from jax.experimental.pallas import tpu as pltpu
 from jax.sharding import PartitionSpec as P
 
 H = 32
@@ -11,7 +15,283 @@
 UNITS = 64
 CHANNELS = 3 * H * DK
 
+GROUP = 4
+SPAN = H * DK // GROUP
+CHUNK = 512
+PER_SPAN = SPAN // CHUNK
+CHUNKS = 3 * PER_SPAN
+LAG = 2
+
 norm_eps = 1e-06
+
+
+def project_kernel(
+    devices,
+    rows,
+    w_ref,
+    gate_ref,
+    tap_ref,
+    toks_ref,
+    out_ref,
+    gate_out_ref,
+    tap_out_ref,
+    land,
+    partial,
+    red,
+    summed,
+    final,
+    gate_land,
+    gate_partial,
+    gate_red,
+    tap_land,
+    own_sem,
+    w_send,
+    w_recv,
+    z_send,
+    z_recv,
+    f_send,
+    f_recv,
+    g_send,
+    g_recv,
+    h_send,
+    h_recv,
+    t_send,
+    t_recv,
+):
+    me = lax.axis_index("heads")
+    outer = devices // GROUP
+    place, inner = me // GROUP, me % GROUP
+    band = GROUP * rows
+
+    def remote(src, dst, send, recv, target):
+        return pltpu.make_async_remote_copy(
+            src_ref=src,
+            dst_ref=dst,
+            send_sem=send,
+            recv_sem=recv,
+            device_id={"heads": target},
+            device_id_type=pl.DeviceIdType.MESH,
+        )
+
+    def mate(k):
+        return place * GROUP + (inner + k) % GROUP
+
+    def across(k):
+        return ((place + k) % outer) * GROUP + inner
+
+    def source_columns(c, owner):
+        start = (c // PER_SPAN) * H * DK + owner * SPAN + (c % PER_SPAN) * CHUNK
+        return pl.ds(pl.multiple_of(start, CHUNK), CHUNK)
+
+    def local_columns(c):
+        return pl.ds(c * CHUNK, CHUNK)
+
+    own = []
+    for c in range(CHUNKS):
+        own.append(
+            pltpu.make_async_copy(
+                w_ref.at[:, source_columns(c, inner)],
+                land.at[0, :, local_columns(c)],
+                own_sem.at[c],
+            )
+        )
+        own[c].start()
+
+    barrier = pltpu.get_barrier_semaphore()
+    for k in range(1, devices):
+        pl.semaphore_signal(
+            barrier,
+            inc=1,
+            device_id={"heads": (me + k) % devices},
+            device_id_type=pl.DeviceIdType.MESH,
+        )
+    pl.semaphore_wait(barrier, devices - 1)
+
+    gates = []
+    for k in range(1, GROUP):
+        gates.append(
+            remote(gate_ref, gate_land.at[k - 1], g_send.at[k - 1], g_recv.at[k - 1], mate(k))
+        )
+        gates[-1].start()
+    spread = []
+    for c in range(CHUNKS):
+        group = []
+        for k in range(1, GROUP):
+            owner = (inner + k) % GROUP
+            group.append(
+                remote(
+                    w_ref.at[:, source_columns(c, owner)],
+                    land.at[k, :, local_columns(c)],
+                    w_send.at[c, k - 1],
+                    w_recv.at[c, k - 1],
+                    mate(k),
+                )
+            )
+            group[-1].start()
+        spread.append(group)
+        if c == 0:
+            taps = []
+            for k in range(1, devices):
+                taps.append(
+                    remote(
+                        tap_ref,
+                        tap_land.at[me],
+                        t_send.at[k - 1],
+                        t_recv.at[k - 1],
+                        (me + k) % devices,
+                    )
+                )
+                taps[-1].start()
+
+    for copy in gates:
+        copy.wait()
+    total = jnp.dot(toks_ref[inner], gate_ref[...], preferred_element_type=jnp.float32)
+    for k in range(1, GROUP):
+        source = (inner + GROUP - k) % GROUP
+        total = total + jnp.dot(
+            toks_ref[source], gate_land[k - 1], preferred_element_type=jnp.float32
+        )
+    gate_partial[...] = total
+    gate_sends = []
+    for k in range(1, outer):
+        start = ((place + k) % outer) * band + inner * rows
+        gate_sends.append(
+            remote(
+                gate_partial.at[pl.ds(pl.multiple_of(start, rows), rows)],
+                gate_red.at[k - 1],
+                h_send.at[k - 1],
+                h_recv.at[k - 1],
+                across(k),
+            )
+        )
+        gate_sends[-1].start()
+
+    my_band = pl.ds(pl.multiple_of(place * band, band), band)
+    crossing = []
+    closing = []
+
+    def finish(c):
+        here = local_columns(c)
+        for copy in crossing[c]:
+            copy.wait()
+        whole = partial[my_band, here]
+        for k in range(1, outer):
+            whole = whole + red[k - 1, :, here]
+        summed[:, here] = whole
+        group = []
+        for k in range(1, GROUP):
+            start = ((inner + k) % GROUP) * rows
+            group.append(
+                remote(
+                    summed.at[pl.ds(pl.multiple_of(start, rows), rows), here],
+                    final.at[k - 1, :, here],
+                    f_send.at[c, k - 1],
+                    f_recv.at[c, k - 1],
+                    mate(k),
+                )
+            )
+            group[-1].start()
+        closing.append(group)
+
+    for c in range(CHUNKS):
+        here = local_columns(c)
+        own[c].wait()
+        for copy in spread[c]:
+            copy.wait_recv()
+        total = jnp.dot(toks_ref[inner], land[0, :, here], preferred_element_type=jnp.float32)
+        for k in range(1, GROUP):
+            source = (inner + GROUP - k) % GROUP
+            total = total + jnp.dot(
+                toks_ref[source], land[k, :, here], preferred_element_type=jnp.float32
+            )
+        partial[:, here] = total
+        group = []
+        for k in range(1, outer):
+            start = ((place + k) % outer) * band
+            group.append(
+                remote(
+                    partial.at[pl.ds(pl.multiple_of(start, band), band), here],
+                    red.at[k - 1, :, here],
+                    z_send.at[c, k - 1],
+                    z_recv.at[c, k - 1],
+                    across(k),
+                )
+            )
+            group[-1].start()
+        crossing.append(group)
+        if c >= LAG:
+            finish(c - LAG)
+    for c in range(CHUNKS - LAG, CHUNKS):
+        finish(c)
+
+    for copy in gate_sends:
+        copy.wait()
+    my_rows = pl.ds(pl.multiple_of(me * rows, rows), rows)
+    gate_total = gate_partial[my_rows, :]
+    for k in range(1, outer):
+        gate_total = gate_total + gate_red[k - 1]
+    gate_out_ref[...] = gate_total
+    for copy in taps:
+        copy.wait()
+    tap_land[me] = tap_ref[...]
+    tap_out_ref[...] = tap_land[...]
+    kept = pl.ds(pl.multiple_of(inner * rows, rows), rows)
+    for c in range(CHUNKS):
+        here = local_columns(c)
+        out_ref[:, source_columns(c, inner)] = summed[kept, here]
+        for k in range(1, GROUP):
+            closing[c][k - 1].wait()
+            source = (inner + GROUP - k) % GROUP
+            out_ref[:, source_columns(c, source)] = final[k - 1, :, here]
+    for group in spread:
+        for copy in group:
+            copy.wait_send()
+
+
+def project(devices, rows, weight, gate, taps, toks):
+    depth = weight.shape[0]
+    outer = devices // GROUP
+    total = devices * rows
+    band = GROUP * rows
+    dma = pltpu.SemaphoreType.DMA
+    vmem = pl.BlockSpec(memory_space=pltpu.VMEM)
+    return pl.pallas_call(
+        functools.partial(project_kernel, devices, rows),
+        out_shape=(
+            jax.ShapeDtypeStruct((rows, CHANNELS), jnp.float32),
+            jax.ShapeDtypeStruct((rows, gate.shape[1]), jnp.float32),
+            jax.ShapeDtypeStruct((devices,) + taps.shape, taps.dtype),
+        ),
+        in_specs=[pl.BlockSpec(memory_space=pl.ANY), vmem, vmem, vmem],
+        out_specs=(vmem, vmem, vmem),
+        scratch_shapes=[
+            pltpu.VMEM((GROUP, depth, 3 * SPAN), jnp.bfloat16),
+            pltpu.VMEM((total, 3 * SPAN), jnp.float32),
+            pltpu.VMEM((outer - 1, band, 3 * SPAN), jnp.float32),
+            pltpu.VMEM((band, 3 * SPAN), jnp.float32),
+            pltpu.VMEM((GROUP - 1, rows, 3 * SPAN), jnp.float32),
+            pltpu.VMEM((GROUP - 1,) + gate.shape, jnp.bfloat16),
+            pltpu.VMEM((total, gate.shape[1]), jnp.float32),
+            pltpu.VMEM((outer - 1, rows, gate.shape[1]), jnp.float32),
+            pltpu.VMEM((devices,) + taps.shape, taps.dtype),
+            dma((CHUNKS,)),
+            dma((CHUNKS, GROUP - 1)),
+            dma((CHUNKS, GROUP - 1)),
+            dma((CHUNKS, outer - 1)),
+            dma((CHUNKS, outer - 1)),
+            dma((CHUNKS, GROUP - 1)),
+            dma((CHUNKS, GROUP - 1)),
+            dma((GROUP - 1,)),
+            dma((GROUP - 1,)),
+            dma((outer - 1,)),
+            dma((outer - 1,)),
+            dma((devices - 1,)),
+            dma((devices - 1,)),
+        ],
+        compiler_params=pltpu.CompilerParams(
+            collective_id=0, has_side_effects=True, vmem_limit_bytes=48 * 1024 * 1024
+        ),
+    )(weight, gate, taps, toks)
 
 
 def unit_positions(old_heads, new_units):
@@ -89,30 +369,26 @@
     row_count = tokens.shape[0]
     rows_dev = delta_state.shape[0]
     depth = qkv_weight.shape[0]
-    taps = lax.all_gather(conv_weight, "heads", axis=1, tiled=True)
-
     row_range = jnp.arange(row_count, dtype=jnp.int32)
     to_old = (slot_of[None, :] == row_range[:, None]).astype(jnp.bfloat16)
     tokens_old = jnp.einsum(
         "ob,bsd->osd", to_old, tokens, preferred_element_type=jnp.float32
     ).astype(jnp.bfloat16)
-    width = tokens.shape[2]
-    columns = H * DK // devices
-    shaped = qkv_weight.reshape(depth, 3, devices, columns)
-    mine_weight = lax.all_to_all(shaped, "heads", split_axis=2, concat_axis=0, tiled=True)
-    projected_all = jnp.dot(
-        tokens_old.reshape(row_count * STEPS, width),
-        mine_weight.reshape(width, 3 * columns),
-        preferred_element_type=jnp.float32,
-    ).reshape(row_count, STEPS, 3, 1, columns)
-    projected = lax.all_to_all(
-        projected_all, "heads", split_axis=0, concat_axis=3, tiled=True
-    ).reshape(rows_dev, STEPS, CHANNELS)
-    gates_all = lax.all_gather(gate_weight, "heads", axis=0, tiled=True)
-    my_tokens = lax.dynamic_slice_in_dim(tokens_old, my_index * rows_dev, rows_dev, 0)
-    gate_pre = jnp.dot(
-        my_tokens.reshape(rows_dev * STEPS, width), gates_all, preferred_element_type=jnp.float32
-    ).reshape(rows_dev, STEPS, 2, H)
+    rows = rows_dev * STEPS
+    place = my_index // GROUP
+    toks = lax.dynamic_slice_in_dim(
+        tokens_old.reshape(row_count * STEPS, tokens.shape[2]),
+        place * GROUP * depth,
+        GROUP * depth,
+        1,
+    )
+    toks = toks.reshape(row_count * STEPS, GROUP, depth).transpose(1, 0, 2)
+    gate_padded = jnp.pad(gate_weight, ((0, 0), (0, 128 - 2 * H)))
+    tap_padded = jnp.pad(conv_weight, ((0, 16 - TAPS), (0, 0)))
+    mine, gate_mine, tap_table = project(devices, rows, qkv_weight, gate_padded, tap_padded, toks)
+    projected = mine.reshape(rows_dev, STEPS, CHANNELS)
+    gate_pre = gate_mine[:, : 2 * H].reshape(rows_dev, STEPS, 2, H)
+    taps = tap_table[:, :TAPS].transpose(1, 0, 2).reshape(TAPS, CHANNELS)
 
     my_slots = my_index * rows_dev + jnp.arange(rows_dev, dtype=jnp.int32)
     live_lengths = jnp.sum(

time: 184 us -> 91.9 us (0.50)
  blocking collectives: 120 us -> 11.2 us
  Pallas kernels: 0 us -> 60.1 us
  local copies, waits for them, and re-layouts: 23.8 us -> 6.76 us
  waiting for transfers between devices: 11.7 us -> 0 us
  starting transfers between devices: 11.3 us -> 0 us
  matrix products: 9.83 us -> 6.81 us
    all_gather x2 -> x0, blocking collectives: 110 us -> none  [the longest x1 76.9 us: on_device(): gates_all = lax.all_gather(gate_weight, 'heads', axis=0, tiled=True)]
    pallas_call x0 -> x1, Pallas kernels: none -> 60.1 us  [project(): pl.pallas_call(functools.partial(project_kernel, devices, rows), out_shap...]
    all_to_all x2 -> x0, waiting for transfers between devices: 11.7 us -> none  [the longest x1 11.6 us: on_device(): lax.all_to_all(projected_all, 'heads', split_axis=0, concat_axis=3, tiled...]
    all_to_all x2 -> x0, starting transfers between devices: 11.3 us -> none  [the longest x1 7.6 us: on_device(): lax.all_to_all(shaped, 'heads', split_axis=2, concat_axis=0, tiled=True)]
    dot_general x2 -> x0, local copies, waits for them, and re-layouts: 6.78 us -> none  [on_device(): jnp.dot(tokens_old.reshape(row_count * STEPS, width), mine_weight.reshape...]
    all_to_all x2 -> x0, local copies, waits for them, and re-layouts: 4.56 us -> none  [the longest x1 4.43 us: on_device(): lax.all_to_all(shaped, 'heads', split_axis=2, concat_axis=0, tiled=True)]
    dot_general x2 -> x0, matrix products: 3.66 us -> none  [the longest x1 3.33 us: on_device(): jnp.dot(tokens_old.reshape(row_count * STEPS, width), mine_weight.reshape...]
    unnamed x23, local copies, waits for them, and re-layouts: 7.01 us -> 3.77 us
  transfers between devices with their start and end apart: 2 -> 0, of which waited for: 1 -> 0; matrix products, arithmetic and copies ran while one was open for 1% -> 0% of each run, Pallas kernels for 0% -> 0%
where the time goes in v2:
time: 91.9 us; the launch traced here: 91.7 us
  Pallas kernels  60.1 us (65%)
  blocking collectives  11.2 us (12%)
  matrix products  6.81 us (7%)
  local copies, waits for them, and re-layouts  6.76 us (7%)
  other arithmetic  6.39 us (7%)
    pallas_call x1, Pallas kernels, project(): pl.pallas_call(functools.partial(project_kernel, devices, rows), out_shap...  60.1 us
    all_to_all x1, blocking collectives, on_device(): lax.all_to_all(units_out, 'heads', split_axis=2, concat_axis=0, tiled=True)  11.2 us
    dot_general x1, matrix products, decode(): jnp.einsum('rihk,rhkv->rihv', both, state, precision=lax.Precision.HIGHEST)  5.29 us
    unnamed x23, local copies, waits for them, and re-layouts  3.77 us
    another operation x3, other arithmetic  2.4 us
    reduce_sum x1, other arithmetic, decode(): overlap = jnp.sum(queries[:, s] * keys[:, j], axis=-1) * spans[j]  2.22 us

profile of v2, /device:TPU:0, one launch (start us, length us, event | category | flops | bytes accessed | tf_op | source)
XLA Modules:
  0.0 91.7 jit_solution(12005365993003562820)
XLA Ops:
  0.0 1.1 %copy-done = bf16[32,4,2304]{2,1,0:T(4,128)(2,1)S(1)} copy-done((bf16[32,4,2304]{2,1,0:T(4,128)(2,1)S(1)}, bf16[32,4,2304]{2,1,0:T(4,128)(2,1)}, u32[]{:S(2)}) %copy-start) | copy-done | bytes 589848
  1.1 1.1 %convolution_convert_fusion = bf16[32,4,2304]{2,0,1:T(8,128)(2,1)S(1)} fusion(bf16[32,4,2304]{2,1,0:T(4,128)(2,1)S(1)} %copy-done, s32[32]{0:T(128)} %param.18), kind=kOutput, calls=%fused_computation | convolution fusion | flops 19170304 | bytes 1179776 | tf_op jit(solution)/shard_map/ob,bsd->osd/dot_general | solution.py:374
  2.2 0.5 copy.63
  2.9 0.1 copy.64
  3.0 0.1 copy.65
  3.4 2.0 %copy-done.1 = bf16[144,12288]{1,0:T(8,128)(2,1)S(1)} copy-done((bf16[144,12288]{1,0:T(8,128)(2,1)S(1)}, bf16[144,12288]{1,0:T(8,128)(2,1)}, u32[]{:S(2)}) %copy-start.1) | copy-done | bytes 3538968
  5.4 60.1 %shard_map.100 = (f32[8,12288]{1,0:T(8,128)S(1)}, f32[8,128]{1,0:T(8,128)S(1)}, bf16[16,16,768]{2,1,0:T(8,128)(2,1)S(1)}) custom-call(bf16[144,12288]{1,0:T(8,128)(2,1)S(1)} %copy-done.1, bf16[144,128]{1,0:T(8,128)(2,1)S(1)} %pad.8.gate_ref, bf16[16,768]{1,0:T(8,128)(2,1)S(1)} %pad.9.tap_ref, bf16[4,128,144]{2,1,0:T(8,128)(2,1)S(1)} %bitcast.117), custom_call_target="tpu_custom_call" | custom-call | tf_op jit(solution)/shard_map/pallas_call | solution.py:258
  65.5 0.1 fusion.76
  65.8 0.2 copy.67
  66.0 0.7 divide_multiply_fusion
  66.8 0.3 reshape.255
  67.1 0.3 multiply_reduce_fusion
  67.8 2.2 %multiply_reduce_fusion.16 = (f32[2,32]{1,0:T(2,128)S(1)}, f32[2,32]{1,0:T(2,128)S(1)}, f32[2,32]{1,0:T(2,128)S(1)}, f32[2,32]{1,0:T(2,128)S(1)}, f32[2,32]{1,0:...) fusion(f32[2,4,32,128]{3,1,2,0:T(4,128)S(1)} %fusion.20, ...), kind=kLoop, calls=%fused_computation.87 | loop fusion | flops 261120 | bytes 266240 | tf_op jit(solution)/shard_map/reduce_sum | solution.py:348
  70.0 5.3 %convolution_bitcast_fusion = f32[2,8,32,128]{3,1,2,0:T(8,128)S(1)} fusion(f32[2,32,128,128]{3,2,1,0:T(8,128)} %param.14, f32[2,4,32,128]{3,1,2,0:T(4,128)S(1)} %fusion.21, f32[2,4,32,128]{3,1,2,0:T(4,128)S(1)} %fusion.20), kind=kOutput, calls=%fused_computation.1 | convolution fusion | flops 100728832 | bytes 4718592 | tf_op jit(solution)/shard_map/rihk,rhkv->rihv/dot_general | solution.py:330
  75.5 0.2 fusion.55
  75.7 0.3 convert_reduce_fusion.3
  76.0 1.0 %convert_reduce_fusion.2 = (bf16[2,32,128]{2,1,0:T(8,128)(2,1)S(1)}, bf16[2,32,128]{2,1,0:T(8,128)(2,1)S(1)}, f32[2,1,32,128]{3,1,2,0:T(1,128)S(1)}) fusion(pred[2]{0:T(512)(128)(4,1)S(1)} %get-tuple-element.76, f32[2,1,32,128]{3,1,2,0:T(1,128)S(1)} %get-tuple-element.30, f32[2,8,32,128]{3,1,2,0:T(8,128)S(1)} %convolution_bitcast_fusion, ...), kind=kLoop, calls=%fused_computation.84 | loop fusion | flops 229376 | bytes 297988 | tf_op jit(solution)/shard_map/convert.7
  77.1 1.1 %convert_reduce_fusion = bf16[2,32,128]{2,1,0:T(8,128)(2,1)S(1)} fusion(f32[2,1,32,128]{3,1,2,0:T(1,128)S(1)} %get-tuple-element.31, f32[2,1,32,128]{3,1,2,0:T(1,128)S(1)} %get-tuple-element.30, f32[2,8,32,128]{3,1,2,0:T(8,128)S(1)} %convolution_bitcast_fusion, f32[2,4,32,128]{3,1,2,0:T(4,128)S(1)} %bitcast.121, pred[2]{0:T(512)(128)(4,1)S(1)} %get-tuple-element.74, ...), kind=kLoop, calls=%fused_computation.70 | loop fusion | flops 221184 | bytes 249090 | tf_op jit(solution)/shard_map/convert.5
  78.7 0.2 fusion
  79.2 11.2 %all_to_all.15 = bf16[16,2,1024]{2,1,0:T(2,128)(2,1)S(1)} all-to-all(bf16[16,2,1024]{2,1,0:T(2,128)(2,1)S(1)} %reshape.264), channel_id=1, replica_groups=mesh['groups'=2,'heads'=16] {'heads'}, dimensions={0} | all-to-all | bytes 131072 | tf_op jit(solution)/shard_map/all_to_all | solution.py:407
  90.5 0.1 reshape.265
  90.7 0.1 reshape.256
  90.8 0.2 convolution_convert_fusion.2
  91.0 0.7 copy.78
  (50 shorter events, 2.0 us)
Async XLA Ops:
  0.0 1.1 %copy-start = (bf16[32,4,2304]{2,1,0:T(4,128)(2,1)S(1)}, bf16[32,4,2304]{2,1,0:T(4,128)(2,1)}, u32[]{:S(2)}) copy-start(bf16[32,4,2304]{2,1,0:T(4,128)(2,1)} %param.10) | copy-start | bytes 1769476
  0.0 3.2 %copy-start.3 = (bf16[144,64]{0,1:T(8,128)(2,1)S(1)}, bf16[144,64]{0,1:T(8,128)(2,1)}, u32[]{:S(2)}) copy-start(bf16[144,64]{0,1:T(8,128)(2,1)} %param.12) | copy-start | bytes 55300
  0.0 3.3 %copy-start.4 = (bf16[4,768]{1,0:T(4,128)(2,1)S(1)}, bf16[4,768]{1,0:T(4,128)(2,1)}, u32[]{:S(2)}) copy-start(bf16[4,768]{1,0:T(4,128)(2,1)} %param.13) | copy-start | bytes 18436
  2.2 63.7 %copy-start.2 = (f32[2,3,12288]{2,0,1:T(2,128)S(1)}, f32[2,3,12288]{2,0,1:T(2,128)}, u32[]{:S(2)}) copy-start(f32[2,3,12288]{2,0,1:T(2,128)} %param.15) | copy-start | bytes 884740
  3.4 2.0 %copy-start.1 = (bf16[144,12288]{1,0:T(8,128)(2,1)S(1)}, bf16[144,12288]{1,0:T(8,128)(2,1)}, u32[]{:S(2)}) copy-start(bf16[144,12288]{1,0:T(8,128)(2,1)} %w_ref.1) | copy-start | bytes 10616836
  66.7 8.7 %copy-start.5 = (s32[32]{0:T(128)S(1)}, s32[32]{0:T(128)}, u32[]{:S(2)}) copy-start(s32[32]{0:T(128)} %param.18) | copy-start | bytes 388
  66.8 8.7 %copy-start.6 = (s32[32]{0:T(128)S(1)}, s32[32]{0:T(128)}, u32[]{:S(2)}) copy-start(s32[32]{0:T(128)} %param.19) | copy-start | bytes 388
  67.0 11.4 %copy-start.8 = (s32[64]{0:T(128)S(1)}, s32[64]{0:T(128)}, u32[]{:S(2)}) copy-start(s32[64]{0:T(128)} %param.17) | copy-start | bytes 772
  67.1 11.4 %copy-start.7 = (s32[32]{0:T(128)S(1)}, s32[32]{0:T(128)}, u32[]{:S(2)}) copy-start(s32[32]{0:T(128)} %param.16) | copy-start | bytes 388

commit v3 on v2

--- a/solution.py
+++ b/solution.py
@@ -17,7 +17,7 @@
 
 GROUP = 4
 SPAN = H * DK // GROUP
-CHUNK = 512
+CHUNK = 256
 PER_SPAN = SPAN // CHUNK
 CHUNKS = 3 * PER_SPAN
 LAG = 2
@@ -294,6 +294,53 @@
     )(weight, gate, taps, toks)
 
 
+def exchange_kernel(devices, blocks_ref, out_ref, land, send, recv):
+    me = lax.axis_index("heads")
+    barrier = pltpu.get_barrier_semaphore()
+    for k in range(1, devices):
+        pl.semaphore_signal(
+            barrier,
+            inc=1,
+            device_id={"heads": (me + k) % devices},
+            device_id_type=pl.DeviceIdType.MESH,
+        )
+    pl.semaphore_wait(barrier, devices - 1)
+    copies = []
+    for k in range(1, devices):
+        target = (me + k) % devices
+        copies.append(
+            pltpu.make_async_remote_copy(
+                src_ref=blocks_ref.at[target],
+                dst_ref=land.at[me],
+                send_sem=send.at[k - 1],
+                recv_sem=recv.at[k - 1],
+                device_id={"heads": target},
+                device_id_type=pl.DeviceIdType.MESH,
+            )
+        )
+        copies[-1].start()
+    land[me] = blocks_ref[me]
+    for copy in copies:
+        copy.wait()
+    out_ref[...] = land[...]
+
+
+def exchange(devices, blocks):
+    vmem = pl.BlockSpec(memory_space=pltpu.VMEM)
+    return pl.pallas_call(
+        functools.partial(exchange_kernel, devices),
+        out_shape=jax.ShapeDtypeStruct(blocks.shape, blocks.dtype),
+        in_specs=[vmem],
+        out_specs=vmem,
+        scratch_shapes=[
+            pltpu.VMEM(blocks.shape, blocks.dtype),
+            pltpu.SemaphoreType.DMA((devices - 1,)),
+            pltpu.SemaphoreType.DMA((devices - 1,)),
+        ],
+        compiler_params=pltpu.CompilerParams(collective_id=1, has_side_effects=True),
+    )(blocks)
+
+
 def unit_positions(old_heads, new_units):
     positions = jnp.arange(H, dtype=jnp.int32)
     inverse = jnp.sum(
@@ -327,7 +374,7 @@
     beta = jax.nn.sigmoid(gate_pre[:, :, 0])
     decay = jnp.exp(-jax.nn.softplus(gate_pre[:, :, 1]))
     both = jnp.concatenate([queries, keys], axis=1)
-    based = jnp.einsum("rihk,rhkv->rihv", both, state, precision=lax.Precision.HIGHEST)
+    based = jnp.einsum("rihk,rhkv->rihv", both, state, precision=lax.Precision.HIGH)
     query_base, key_base = based[:, :STEPS], based[:, STEPS:]
 
     corrections = []
@@ -371,18 +418,13 @@
     depth = qkv_weight.shape[0]
     row_range = jnp.arange(row_count, dtype=jnp.int32)
     to_old = (slot_of[None, :] == row_range[:, None]).astype(jnp.bfloat16)
-    tokens_old = jnp.einsum(
-        "ob,bsd->osd", to_old, tokens, preferred_element_type=jnp.float32
-    ).astype(jnp.bfloat16)
     rows = rows_dev * STEPS
     place = my_index // GROUP
-    toks = lax.dynamic_slice_in_dim(
-        tokens_old.reshape(row_count * STEPS, tokens.shape[2]),
-        place * GROUP * depth,
-        GROUP * depth,
-        1,
-    )
-    toks = toks.reshape(row_count * STEPS, GROUP, depth).transpose(1, 0, 2)
+    my_tokens = lax.dynamic_slice_in_dim(tokens, place * GROUP * depth, GROUP * depth, 2)
+    tokens_old = jnp.einsum(
+        "ob,bsd->osd", to_old, my_tokens, preferred_element_type=jnp.float32
+    ).astype(jnp.bfloat16)
+    toks = tokens_old.reshape(row_count * STEPS, GROUP, depth).transpose(1, 0, 2)
     gate_padded = jnp.pad(gate_weight, ((0, 0), (0, 128 - 2 * H)))
     tap_padded = jnp.pad(conv_weight, ((0, 16 - TAPS), (0, 0)))
     mine, gate_mine, tap_table = project(devices, rows, qkv_weight, gate_padded, tap_padded, toks)
@@ -404,7 +446,8 @@
         pick,
         preferred_element_type=jnp.float32,
     ).astype(jnp.bfloat16)
-    outputs_old = lax.all_to_all(units_out, "heads", split_axis=2, concat_axis=0, tiled=True)
+    blocks = units_out.reshape(rows, devices, (UNITS // devices) * HALF).transpose(1, 0, 2)
+    outputs_old = exchange(devices, blocks)
     flat_old = outputs_old.reshape(row_count, STEPS, (UNITS // devices) * HALF)
     return jnp.einsum(
         "ob,osc->bsc", to_old, flat_old, preferred_element_type=jnp.float32

time: 91.9 us -> 88.9 us (0.967)
  blocking collectives: 11.2 us -> 0 us
  Pallas kernels: 60.1 us -> 68.2 us
  local copies, waits for them, and re-layouts: 6.76 us -> 8.79 us
  matrix products: 6.81 us -> 4.85 us
    all_to_all x1 -> x0, blocking collectives: 11.2 us -> none  [on_device(): lax.all_to_all(units_out, 'heads', split_axis=2, concat_axis=0, tiled=True)]
    pallas_call x0 -> x1, Pallas kernels: none -> 8.15 us  [exchange(): pl.pallas_call(functools.partial(exchange_kernel, devices), out_shape=jax...]
    dot_general x2, matrix products: 6.38 us -> 4.41 us  [the longest x1 3.45 us: decode(): jnp.einsum('rihk,rhkv->rihv', both, state, precision=lax.Precision.HIGH)]
    unnamed x23 -> x17, local copies, waits for them, and re-layouts: 3.77 us -> 4.25 us
where the time goes in v3:
time: 88.9 us; the launch traced here: 88.5 us
  Pallas kernels  68.2 us (77%)
  local copies, waits for them, and re-layouts  8.79 us (10%)
  other arithmetic  6.37 us (7%)
  matrix products  4.85 us (5%)
    pallas_call x1, Pallas kernels, project(): pl.pallas_call(functools.partial(project_kernel, devices, rows), out_shap...  60 us
    pallas_call x1, Pallas kernels, exchange(): pl.pallas_call(functools.partial(exchange_kernel, devices), out_shape=jax...  8.15 us
    unnamed x17, local copies, waits for them, and re-layouts  4.25 us
    dot_general x1, matrix products, decode(): jnp.einsum('rihk,rhkv->rihv', both, state, precision=lax.Precision.HIGH)  3.45 us
    another operation x3, other arithmetic  2.4 us
    reduce_sum x1, other arithmetic, decode(): overlap = jnp.sum(queries[:, s] * keys[:, j], axis=-1) * spans[j]  2.22 us

profile of v3, /device:TPU:0, one launch (start us, length us, event | category | flops | bytes accessed | tf_op | source)
XLA Modules:
  0.0 88.5 jit_solution(13160057074092193963)
XLA Ops:
  0.0 1.1 %copy-done = bf16[32,4,2304]{2,1,0:T(4,128)(2,1)S(1)} copy-done((bf16[32,4,2304]{2,1,0:T(4,128)(2,1)S(1)}, bf16[32,4,2304]{2,1,0:T(4,128)(2,1)}, u32[]{:S(2)}) %copy-start) | copy-done | bytes 589848
  1.1 0.2 constant_dynamic-slice_fusion
  1.2 1.0 %convolution_convert_fusion = bf16[32,4,576]{2,0,1:T(8,128)(2,1)S(1)} fusion(bf16[32,4,576]{2,1,0:T(4,128)(2,1)S(1)} %constant_dynamic-slice_fusion, s32[32]{0:T(128)} %param.18), kind=kOutput, calls=%fused_computation.1 | convolution fusion | flops 4793344 | bytes 295040 | tf_op jit(solution)/shard_map/ob,bsd->osd/dot_general | solution.py:424
  2.3 0.2 reshape.250
  2.5 0.9 copy.41
  3.4 0.7 pad.9.tap_ref
  4.1 2.0 %copy-done.1 = bf16[144,12288]{1,0:T(8,128)(2,1)S(1)} copy-done((bf16[144,12288]{1,0:T(8,128)(2,1)S(1)}, bf16[144,12288]{1,0:T(8,128)(2,1)}, u32[]{:S(2)}) %copy-start.1) | copy-done | bytes 3538968
  6.1 60.0 %shard_map.100 = (f32[8,12288]{1,0:T(8,128)S(1)}, f32[8,128]{1,0:T(8,128)S(1)}, bf16[16,16,768]{2,1,0:T(8,128)(2,1)S(1)}) custom-call(bf16[144,12288]{1,0:T(8,128)(2,1)S(1)} %copy-done.1, bf16[144,128]{1,0:T(8,128)(2,1)S(1)} %pad.8.gate_ref, bf16[16,768]{1,0:T(8,128)(2,1)S(1)} %pad.9.tap_ref, bf16[4,128,144]{2,1,0:T(8,128)(2,1)S(1)} %bitcast.112), custom_call_target="tpu_custom_call" | custom-call | tf_op jit(solution)/shard_map/pallas_call | solution.py:258
  66.5 0.2 copy.47
  66.7 0.7 divide_multiply_fusion
  67.4 0.3 reshape.253
  67.8 0.3 multiply_reduce_fusion
  68.3 2.2 %multiply_reduce_fusion.16 = (f32[2,32]{1,0:T(2,128)S(1)}, f32[2,32]{1,0:T(2,128)S(1)}, f32[2,32]{1,0:T(2,128)S(1)}, f32[2,32]{1,0:T(2,128)S(1)}, f32[2,32]{1,0:...) fusion(f32[2,4,32,128]{3,1,2,0:T(4,128)S(1)} %fusion.20, ...), kind=kLoop, calls=%fused_computation.89 | loop fusion | flops 261120 | bytes 266240 | tf_op jit(solution)/shard_map/reduce_sum | solution.py:395
  70.7 3.4 %convolution_bitcast_fusion = f32[2,8,32,128]{3,1,2,0:T(8,128)S(1)} fusion(f32[2,32,128,128]{3,2,1,0:T(8,128)} %param.14, f32[2,4,32,128]{3,1,2,0:T(4,128)S(1)} %fusion.21, f32[2,4,32,128]{3,1,2,0:T(4,128)S(1)} %fusion.20), kind=kOutput, calls=%fused_computation | convolution fusion | flops 50397184 | bytes 4718592 | tf_op jit(solution)/shard_map/rihk,rhkv->rihv/dot_general | solution.py:377
  74.3 0.2 fusion.56
  74.5 0.3 convert_reduce_fusion.3
  74.8 1.0 %convert_reduce_fusion.2 = (bf16[2,32,128]{2,1,0:T(8,128)(2,1)S(1)}, bf16[2,32,128]{2,1,0:T(8,128)(2,1)S(1)}, f32[2,1,32,128]{3,1,2,0:T(1,128)S(1)}) fusion(pred[2]{0:T(512)(128)(4,1)S(1)} %get-tuple-element.76, f32[2,1,32,128]{3,1,2,0:T(1,128)S(1)} %get-tuple-element.30, f32[2,8,32,128]{3,1,2,0:T(8,128)S(1)} %convolution_bitcast_fusion, ...), kind=kLoop, calls=%fused_computation.86 | loop fusion | flops 229376 | bytes 297988 | tf_op jit(solution)/shard_map/convert.7
  75.9 1.1 %convert_reduce_fusion = bf16[2,32,128]{2,1,0:T(8,128)(2,1)S(1)} fusion(f32[2,1,32,128]{3,1,2,0:T(1,128)S(1)} %get-tuple-element.31, f32[2,1,32,128]{3,1,2,0:T(1,128)S(1)} %get-tuple-element.30, f32[2,8,32,128]{3,1,2,0:T(8,128)S(1)} %convolution_bitcast_fusion, f32[2,4,32,128]{3,1,2,0:T(4,128)S(1)} %bitcast.116, pred[2]{0:T(512)(128)(4,1)S(1)} %get-tuple-element.74, ...), kind=kLoop, calls=%fused_computation.72 | loop fusion | flops 221184 | bytes 249090 | tf_op jit(solution)/shard_map/convert.5
  77.5 0.2 fusion
  77.9 0.7 copy.99
  78.6 8.1 %shard_map.101 = bf16[16,8,256]{2,1,0:T(8,128)(2,1)} custom-call(bf16[16,8,256]{2,1,0:T(8,128)(2,1)} %bitcast.117), custom_call_target="tpu_custom_call" | custom-call | tf_op jit(solution)/shard_map/pallas_call | solution.py:330
  86.7 0.9 reshape.255
  87.6 0.2 convolution_convert_fusion.2
  87.8 0.7 copy.58
  (43 shorter events, 1.7 us)
Async XLA Ops:
  0.0 1.1 %copy-start = (bf16[32,4,2304]{2,1,0:T(4,128)(2,1)S(1)}, bf16[32,4,2304]{2,1,0:T(4,128)(2,1)}, u32[]{:S(2)}) copy-start(bf16[32,4,2304]{2,1,0:T(4,128)(2,1)} %param.10) | copy-start | bytes 1769476
  0.0 66.5 %copy-start.2 = (f32[2,3,12288]{2,0,1:T(2,128)S(1)}, f32[2,3,12288]{2,0,1:T(2,128)}, u32[]{:S(2)}) copy-start(f32[2,3,12288]{2,0,1:T(2,128)} %param.15) | copy-start | bytes 884740
  4.1 2.0 %copy-start.1 = (bf16[144,12288]{1,0:T(8,128)(2,1)S(1)}, bf16[144,12288]{1,0:T(8,128)(2,1)}, u32[]{:S(2)}) copy-start(bf16[144,12288]{1,0:T(8,128)(2,1)} %w_ref.1) | copy-start | bytes 10616836
  67.4 6.9 %copy-start.3 = (s32[32]{0:T(128)S(1)}, s32[32]{0:T(128)}, u32[]{:S(2)}) copy-start(s32[32]{0:T(128)} %param.18) | copy-start | bytes 388
  67.4 6.9 %copy-start.4 = (s32[32]{0:T(128)S(1)}, s32[32]{0:T(128)}, u32[]{:S(2)}) copy-start(s32[32]{0:T(128)} %param.19) | copy-start | bytes 388
  67.7 9.6 %copy-start.6 = (s32[64]{0:T(128)S(1)}, s32[64]{0:T(128)}, u32[]{:S(2)}) copy-start(s32[64]{0:T(128)} %param.17) | copy-start | bytes 772
  67.7 9.6 %copy-start.5 = (s32[32]{0:T(128)S(1)}, s32[32]{0:T(128)}, u32[]{:S(2)}) copy-start(s32[32]{0:T(128)} %param.16) | copy-start | bytes 388

commit v4 on v3

--- a/solution.py
+++ b/solution.py
@@ -20,7 +20,7 @@
 CHUNK = 256
 PER_SPAN = SPAN // CHUNK
 CHUNKS = 3 * PER_SPAN
-LAG = 2
+LAG = 4
 
 norm_eps = 1e-06
 
@@ -129,19 +129,14 @@
             )
             group[-1].start()
         spread.append(group)
-        if c == 0:
-            taps = []
-            for k in range(1, devices):
-                taps.append(
-                    remote(
-                        tap_ref,
-                        tap_land.at[me],
-                        t_send.at[k - 1],
-                        t_recv.at[k - 1],
-                        (me + k) % devices,
-                    )
-                )
-                taps[-1].start()
+    taps = []
+    for k in range(1, devices):
+        taps.append(
+            remote(
+                tap_ref, tap_land.at[me], t_send.at[k - 1], t_recv.at[k - 1], (me + k) % devices
+            )
+        )
+        taps[-1].start()
 
     for copy in gates:
         copy.wait()
@@ -262,7 +257,7 @@
             jax.ShapeDtypeStruct((rows, gate.shape[1]), jnp.float32),
             jax.ShapeDtypeStruct((devices,) + taps.shape, taps.dtype),
         ),
-        in_specs=[pl.BlockSpec(memory_space=pl.ANY), vmem, vmem, vmem],
+        in_specs=[pl.BlockSpec(memory_space=pltpu.HBM), vmem, vmem, vmem],
         out_specs=(vmem, vmem, vmem),
         scratch_shapes=[
             pltpu.VMEM((GROUP, depth, 3 * SPAN), jnp.bfloat16),
@@ -426,11 +421,10 @@
     ).astype(jnp.bfloat16)
     toks = tokens_old.reshape(row_count * STEPS, GROUP, depth).transpose(1, 0, 2)
     gate_padded = jnp.pad(gate_weight, ((0, 0), (0, 128 - 2 * H)))
-    tap_padded = jnp.pad(conv_weight, ((0, 16 - TAPS), (0, 0)))
-    mine, gate_mine, tap_table = project(devices, rows, qkv_weight, gate_padded, tap_padded, toks)
+    mine, gate_mine, tap_table = project(devices, rows, qkv_weight, gate_padded, conv_weight, toks)
     projected = mine.reshape(rows_dev, STEPS, CHANNELS)
     gate_pre = gate_mine[:, : 2 * H].reshape(rows_dev, STEPS, 2, H)
-    taps = tap_table[:, :TAPS].transpose(1, 0, 2).reshape(TAPS, CHANNELS)
+    taps = tap_table.transpose(1, 0, 2).reshape(TAPS, CHANNELS)
 
     my_slots = my_index * rows_dev + jnp.arange(rows_dev, dtype=jnp.int32)
     live_lengths = jnp.sum(

time: 88.9 us -> 85.4 us (0.961)
  Pallas kernels: 68.2 us -> 64.7 us
    pallas_call x1, Pallas kernels: 60 us -> 56.6 us  [project(): pl.pallas_call(functools.partial(project_kernel, devices, rows), out_shap...]
    unnamed x17 -> x19, local copies, waits for them, and re-layouts: 4.25 us -> 4.94 us
where the time goes in v4:
time: 85.4 us; the launch traced here: 85.1 us
  Pallas kernels  64.7 us (76%)
  local copies, waits for them, and re-layouts  8.77 us (10%)
  other arithmetic  6.36 us (7%)
  matrix products  4.85 us (6%)
    pallas_call x1, Pallas kernels, project(): pl.pallas_call(functools.partial(project_kernel, devices, rows), out_shap...  56.6 us
    pallas_call x1, Pallas kernels, exchange(): pl.pallas_call(functools.partial(exchange_kernel, devices), out_shape=jax...  8.14 us
    unnamed x19, local copies, waits for them, and re-layouts  4.94 us
    dot_general x1, matrix products, decode(): jnp.einsum('rihk,rhkv->rihv', both, state, precision=lax.Precision.HIGH)  3.45 us
    another operation x3, other arithmetic  2.4 us
    reduce_sum x1, other arithmetic, decode(): overlap = jnp.sum(queries[:, s] * keys[:, j], axis=-1) * spans[j]  2.22 us

profile of v4, /device:TPU:0, one launch (start us, length us, event | category | flops | bytes accessed | tf_op | source)
XLA Modules:
  0.0 85.1 jit_solution(6612805350714047208)
XLA Ops:
  0.0 1.1 %copy-done = bf16[32,4,2304]{2,1,0:T(4,128)(2,1)S(1)} copy-done((bf16[32,4,2304]{2,1,0:T(4,128)(2,1)S(1)}, bf16[32,4,2304]{2,1,0:T(4,128)(2,1)}, u32[]{:S(2)}) %copy-start) | copy-done | bytes 589848
  1.1 0.2 constant_dynamic-slice_fusion
  1.2 1.0 %convolution_convert_fusion = bf16[32,4,576]{2,0,1:T(8,128)(2,1)S(1)} fusion(bf16[32,4,576]{2,1,0:T(4,128)(2,1)S(1)} %constant_dynamic-slice_fusion, s32[32]{0:T(128)} %param.18), kind=kOutput, calls=%fused_computation.1 | convolution fusion | flops 4793344 | bytes 295040 | tf_op jit(solution)/shard_map/ob,bsd->osd/dot_general | solution.py:419
  2.3 0.2 reshape.250
  2.5 0.9 %copy.41 = bf16[144,64]{1,0:T(8,128)(2,1)S(1)} copy(bf16[144,64]{0,1:T(8,128)(2,1)} %param.12) | data formatting | bytes 36864 | tf_op args[2]
  3.5 2.0 %copy-done.1 = bf16[144,12288]{1,0:T(8,128)(2,1)S(1)} copy-done((bf16[144,12288]{1,0:T(8,128)(2,1)S(1)}, bf16[144,12288]{1,0:T(8,128)(2,1)}, u32[]{:S(2)}) %copy-start.1) | copy-done | bytes 3538968
  5.5 0.7 copy-done.2
  6.1 56.6 %shard_map.100 = (f32[8,12288]{1,0:T(8,128)S(1)}, f32[8,128]{1,0:T(8,128)S(1)}, bf16[16,4,768]{2,1,0:T(4,128)(2,1)S(1)}) custom-call(bf16[144,12288]{1,0:T(8,128)(2,1)S(1)} %copy-done.1, bf16[144,128]{1,0:T(8,128)(2,1)S(1)} %pad.4.gate_ref, bf16[4,768]{1,0:T(4,128)(2,1)S(1)} %copy-done.2, bf16[4,128,144]{2,1,0:T(8,128)(2,1)S(1)} %bitcast.112), custom_call_target="tpu_custom_call" | custom-call | tf_op jit(solution)/shard_map/pallas_call | solution.py:253
  63.0 0.2 copy.47
  63.3 0.7 divide_multiply_fusion
  64.0 0.3 reshape.253
  64.3 0.3 multiply_reduce_fusion
  64.9 2.2 %multiply_reduce_fusion.16 = (f32[2,32]{1,0:T(2,128)S(1)}, f32[2,32]{1,0:T(2,128)S(1)}, f32[2,32]{1,0:T(2,128)S(1)}, f32[2,32]{1,0:T(2,128)S(1)}, f32[2,32]{1,0:...) fusion(f32[2,4,32,128]{3,1,2,0:T(4,128)S(1)} %fusion.20, ...), kind=kLoop, calls=%fused_computation.89 | loop fusion | flops 261120 | bytes 266240 | tf_op jit(solution)/shard_map/reduce_sum | solution.py:390
  67.3 3.4 %convolution_bitcast_fusion = f32[2,8,32,128]{3,1,2,0:T(8,128)S(1)} fusion(f32[2,32,128,128]{3,2,1,0:T(8,128)} %param.14, f32[2,4,32,128]{3,1,2,0:T(4,128)S(1)} %fusion.21, f32[2,4,32,128]{3,1,2,0:T(4,128)S(1)} %fusion.20), kind=kOutput, calls=%fused_computation | convolution fusion | flops 50397184 | bytes 4718592 | tf_op jit(solution)/shard_map/rihk,rhkv->rihv/dot_general | solution.py:372
  70.9 0.2 fusion.56
  71.1 0.3 convert_reduce_fusion.3
  71.4 1.0 %convert_reduce_fusion.2 = (bf16[2,32,128]{2,1,0:T(8,128)(2,1)S(1)}, bf16[2,32,128]{2,1,0:T(8,128)(2,1)S(1)}, f32[2,1,32,128]{3,1,2,0:T(1,128)S(1)}) fusion(pred[2]{0:T(512)(128)(4,1)S(1)} %get-tuple-element.76, f32[2,1,32,128]{3,1,2,0:T(1,128)S(1)} %get-tuple-element.30, f32[2,8,32,128]{3,1,2,0:T(8,128)S(1)} %convolution_bitcast_fusion, ...), kind=kLoop, calls=%fused_computation.86 | loop fusion | flops 229376 | bytes 297988 | tf_op jit(solution)/shard_map/convert.7
  72.4 1.1 %convert_reduce_fusion = bf16[2,32,128]{2,1,0:T(8,128)(2,1)S(1)} fusion(f32[2,1,32,128]{3,1,2,0:T(1,128)S(1)} %get-tuple-element.31, f32[2,1,32,128]{3,1,2,0:T(1,128)S(1)} %get-tuple-element.30, f32[2,8,32,128]{3,1,2,0:T(8,128)S(1)} %convolution_bitcast_fusion, f32[2,4,32,128]{3,1,2,0:T(4,128)S(1)} %bitcast.116, pred[2]{0:T(512)(128)(4,1)S(1)} %get-tuple-element.74, ...), kind=kLoop, calls=%fused_computation.72 | loop fusion | flops 221184 | bytes 249090 | tf_op jit(solution)/shard_map/convert.5
  74.1 0.2 fusion
  74.5 0.7 copy.99
  75.1 8.1 %shard_map.101 = bf16[16,8,256]{2,1,0:T(8,128)(2,1)} custom-call(bf16[16,8,256]{2,1,0:T(8,128)(2,1)} %bitcast.117), custom_call_target="tpu_custom_call" | custom-call | tf_op jit(solution)/shard_map/pallas_call | solution.py:325
  83.3 0.9 %reshape.255 = bf16[32,4,256]{2,1,0:T(4,128)(2,1)S(1)} reshape(bf16[16,8,256]{2,1,0:T(8,128)(2,1)} %shard_map.101) | data formatting | bytes 131072 | tf_op jit(solution)/shard_map/reshape | solution.py:445
  84.2 0.2 convolution_convert_fusion.2
  84.4 0.7 copy.58
  (44 shorter events, 1.7 us)
Async XLA Ops:
  0.0 1.1 %copy-start = (bf16[32,4,2304]{2,1,0:T(4,128)(2,1)S(1)}, bf16[32,4,2304]{2,1,0:T(4,128)(2,1)}, u32[]{:S(2)}) copy-start(bf16[32,4,2304]{2,1,0:T(4,128)(2,1)} %param.10) | copy-start | bytes 1769476
  0.0 63.0 %copy-start.3 = (f32[2,3,12288]{2,0,1:T(2,128)S(1)}, f32[2,3,12288]{2,0,1:T(2,128)}, u32[]{:S(2)}) copy-start(f32[2,3,12288]{2,0,1:T(2,128)} %param.15) | copy-start | bytes 884740
  3.4 2.0 %copy-start.1 = (bf16[144,12288]{1,0:T(8,128)(2,1)S(1)}, bf16[144,12288]{1,0:T(8,128)(2,1)}, u32[]{:S(2)}) copy-start(bf16[144,12288]{1,0:T(8,128)(2,1)} %w_ref.1) | copy-start | bytes 10616836
  5.4 0.7 copy-start.2
  64.0 6.9 %copy-start.4 = (s32[32]{0:T(128)S(1)}, s32[32]{0:T(128)}, u32[]{:S(2)}) copy-start(s32[32]{0:T(128)} %param.18) | copy-start | bytes 388
  64.0 6.9 %copy-start.5 = (s32[32]{0:T(128)S(1)}, s32[32]{0:T(128)}, u32[]{:S(2)}) copy-start(s32[32]{0:T(128)} %param.19) | copy-start | bytes 388
  64.3 9.6 %copy-start.7 = (s32[64]{0:T(128)S(1)}, s32[64]{0:T(128)}, u32[]{:S(2)}) copy-start(s32[64]{0:T(128)} %param.17) | copy-start | bytes 772
  64.3 9.6 %copy-start.6 = (s32[32]{0:T(128)S(1)}, s32[32]{0:T(128)}, u32[]{:S(2)}) copy-start(s32[32]{0:T(128)} %param.16) | copy-start | bytes 388

commit v5 on v4

--- a/solution.py
+++ b/solution.py
@@ -284,7 +284,7 @@
             dma((devices - 1,)),
         ],
         compiler_params=pltpu.CompilerParams(
-            collective_id=0, has_side_effects=True, vmem_limit_bytes=48 * 1024 * 1024
+            collective_id=0, has_side_effects=True, vmem_limit_bytes=61 * 1024 * 1024
         ),
     )(weight, gate, taps, toks)
 

time: 85.4 us -> 87.5 us (1.025)
  Pallas kernels: 64.7 us -> 66.3 us
  other arithmetic: 6.36 us -> 7.26 us
    unnamed x19 -> x17, local copies, waits for them, and re-layouts: 4.94 us -> 2.25 us
    pallas_call x1, Pallas kernels: 56.6 us -> 58.1 us  [project(): pl.pallas_call(functools.partial(project_kernel, devices, rows), out_shap...]
    reshape x1, local copies, waits for them, and re-layouts: 0.11 us -> 1.11 us  [on_device(): projected = mine.reshape(rows_dev, STEPS, CHANNELS)]
    convert_element_type x1, other arithmetic: 0.02 us -> 0.91 us  [decode(): weights_f = taps.astype(jnp.float32)]
where the time goes in v5:
time: 87.5 us; the launch traced here: 87.1 us
  Pallas kernels  66.3 us (76%)
  local copies, waits for them, and re-layouts  8.4 us (10%)
  other arithmetic  7.26 us (8%)
  matrix products  4.85 us (6%)
    pallas_call x1, Pallas kernels, project(): pl.pallas_call(functools.partial(project_kernel, devices, rows), out_shap...  58.1 us
    pallas_call x1, Pallas kernels, exchange(): pl.pallas_call(functools.partial(exchange_kernel, devices), out_shape=jax...  8.14 us
    dot_general x1, matrix products, decode(): jnp.einsum('rihk,rhkv->rihv', both, state, precision=lax.Precision.HIGH)  3.45 us
    another operation x3, other arithmetic  2.4 us
    unnamed x17, local copies, waits for them, and re-layouts  2.25 us
    reduce_sum x1, other arithmetic, decode(): overlap = jnp.sum(queries[:, s] * keys[:, j], axis=-1) * spans[j]  2.22 us

profile of v5, /device:TPU:0, one launch (start us, length us, event | category | flops | bytes accessed | tf_op | source)
XLA Modules:
  0.0 87.1 jit_solution(16226148427896272680)
XLA Ops:
  0.0 1.1 %copy-done = bf16[32,4,2304]{2,1,0:T(4,128)(2,1)S(1)} copy-done((bf16[32,4,2304]{2,1,0:T(4,128)(2,1)S(1)}, bf16[32,4,2304]{2,1,0:T(4,128)(2,1)}, u32[]{:S(2)}) %copy-start) | copy-done | bytes 589848
  1.2 1.0 %convolution_convert_fusion = bf16[32,4,576]{2,0,1:T(8,128)(2,1)S(1)} fusion(bf16[32,4,576]{2,1,0:T(4,128)(2,1)S(1)} %constant_dynamic-slice_fusion, s32[32]{0:T(128)} %param.18), kind=kOutput, calls=%fused_computation.1 | convolution fusion | flops 4793344 | bytes 295040 | tf_op jit(solution)/shard_map/ob,bsd->osd/dot_general | solution.py:419
  2.3 0.2 reshape.250
  2.5 0.7 copy.97
  3.2 0.9 copy.41
  4.1 0.6 pad.4.gate_ref
  4.7 58.1 %shard_map.100 = (f32[8,12288]{1,0:T(8,128)}, f32[8,128]{1,0:T(8,128)}, bf16[16,4,768]{2,1,0:T(4,128)(2,1)}) custom-call(bf16[144,12288]{1,0:T(8,128)(2,1)} %w_ref.1, bf16[144,128]{1,0:T(8,128)(2,1)} %pad.4.gate_ref, bf16[4,768]{1,0:T(4,128)(2,1)} %tap_ref.1, bf16[4,128,144]{2,1,0:T(8,128)(2,1)} %bitcast.112), custom_call_target="tpu_custom_call" | custom-call | tf_op jit(solution)/shard_map/pallas_call | solution.py:253
  62.9 0.9 %convert_bitcast_fusion = f32[4,16,768]{2,0,1:T(4,128)S(1)} fusion(bf16[16,4,768]{2,1,0:T(4,128)(2,1)} %get-tuple-element.9), kind=kLoop, calls=%fused_computation.23 | loop fusion | flops 49152 | bytes 294912 | tf_op jit(solution)/shard_map/convert_element_type | solution.py:358
  64.0 1.1 %reshape.252 = f32[2,4,12288]{2,1,0:T(4,128)S(1)} reshape(f32[8,12288]{1,0:T(8,128)} %get-tuple-element.10) | data formatting | bytes 786432 | tf_op jit(solution)/shard_map/reshape | solution.py:425
  65.1 0.2 copy.47
  65.3 0.7 divide_multiply_fusion
  66.0 0.3 reshape.253
  66.4 0.3 multiply_reduce_fusion
  66.9 2.2 %multiply_reduce_fusion.16 = (f32[2,32]{1,0:T(2,128)S(1)}, f32[2,32]{1,0:T(2,128)S(1)}, f32[2,32]{1,0:T(2,128)S(1)}, f32[2,32]{1,0:T(2,128)S(1)}, f32[2,32]{1,0:...) fusion(f32[2,4,32,128]{3,1,2,0:T(4,128)S(1)} %fusion.20, ...), kind=kLoop, calls=%fused_computation.89 | loop fusion | flops 261120 | bytes 266240 | tf_op jit(solution)/shard_map/reduce_sum | solution.py:390
  69.3 3.4 %convolution_bitcast_fusion = f32[2,8,32,128]{3,1,2,0:T(8,128)S(1)} fusion(f32[2,32,128,128]{3,2,1,0:T(8,128)} %param.14, f32[2,4,32,128]{3,1,2,0:T(4,128)S(1)} %fusion.21, f32[2,4,32,128]{3,1,2,0:T(4,128)S(1)} %fusion.20), kind=kOutput, calls=%fused_computation | convolution fusion | flops 50397184 | bytes 4718592 | tf_op jit(solution)/shard_map/rihk,rhkv->rihv/dot_general | solution.py:372
  73.1 0.3 convert_reduce_fusion.3
  73.4 1.0 %convert_reduce_fusion.2 = (bf16[2,32,128]{2,1,0:T(8,128)(2,1)S(1)}, bf16[2,32,128]{2,1,0:T(8,128)(2,1)S(1)}, f32[2,1,32,128]{3,1,2,0:T(1,128)S(1)}) fusion(pred[2]{0:T(512)(128)(4,1)S(1)} %get-tuple-element.76, f32[2,1,32,128]{3,1,2,0:T(1,128)S(1)} %get-tuple-element.30, f32[2,8,32,128]{3,1,2,0:T(8,128)S(1)} %convolution_bitcast_fusion, ...), kind=kLoop, calls=%fused_computation.86 | loop fusion | flops 229376 | bytes 297988 | tf_op jit(solution)/shard_map/convert.7
  74.5 1.1 %convert_reduce_fusion = bf16[2,32,128]{2,1,0:T(8,128)(2,1)S(1)} fusion(f32[2,1,32,128]{3,1,2,0:T(1,128)S(1)} %get-tuple-element.31, f32[2,1,32,128]{3,1,2,0:T(1,128)S(1)} %get-tuple-element.30, f32[2,8,32,128]{3,1,2,0:T(8,128)S(1)} %convolution_bitcast_fusion, f32[2,4,32,128]{3,1,2,0:T(4,128)S(1)} %bitcast.115, pred[2]{0:T(512)(128)(4,1)S(1)} %get-tuple-element.74, ...), kind=kLoop, calls=%fused_computation.72 | loop fusion | flops 221184 | bytes 249090 | tf_op jit(solution)/shard_map/convert.5
  76.1 0.2 fusion
  76.5 0.7 copy.99
  77.2 8.1 %shard_map.101 = bf16[16,8,256]{2,1,0:T(8,128)(2,1)} custom-call(bf16[16,8,256]{2,1,0:T(8,128)(2,1)} %bitcast.116), custom_call_target="tpu_custom_call" | custom-call | tf_op jit(solution)/shard_map/pallas_call | solution.py:325
  85.3 0.9 reshape.255
  86.2 0.2 convolution_convert_fusion.2
  86.4 0.7 copy.58
  (42 shorter events, 1.9 us)
Async XLA Ops:
  0.0 1.1 %copy-start = (bf16[32,4,2304]{2,1,0:T(4,128)(2,1)S(1)}, bf16[32,4,2304]{2,1,0:T(4,128)(2,1)}, u32[]{:S(2)}) copy-start(bf16[32,4,2304]{2,1,0:T(4,128)(2,1)} %param.10) | copy-start | bytes 1769476
  0.0 65.1 %copy-start.1 = (f32[2,3,12288]{2,0,1:T(2,128)S(1)}, f32[2,3,12288]{2,0,1:T(2,128)}, u32[]{:S(2)}) copy-start(f32[2,3,12288]{2,0,1:T(2,128)} %param.15) | copy-start | bytes 884740
  62.9 6.3 %copy-start.3 = (f32[8,128]{1,0:T(8,128)S(1)}, f32[8,128]{1,0:T(8,128)}, u32[]{:S(2)}) copy-start(f32[8,128]{1,0:T(8,128)} %get-tuple-element.8) | copy-start | bytes 12292
  66.0 6.9 %copy-start.2 = (s32[32]{0:T(128)S(1)}, s32[32]{0:T(128)}, u32[]{:S(2)}) copy-start(s32[32]{0:T(128)} %param.18) | copy-start | bytes 388
  66.0 6.9 %copy-start.4 = (s32[32]{0:T(128)S(1)}, s32[32]{0:T(128)}, u32[]{:S(2)}) copy-start(s32[32]{0:T(128)} %param.19) | copy-start | bytes 388
  66.3 9.6 %copy-start.6 = (s32[64]{0:T(128)S(1)}, s32[64]{0:T(128)}, u32[]{:S(2)}) copy-start(s32[64]{0:T(128)} %param.17) | copy-start | bytes 772
  66.3 9.6 %copy-start.5 = (s32[32]{0:T(128)S(1)}, s32[32]{0:T(128)}, u32[]{:S(2)}) copy-start(s32[32]{0:T(128)} %param.16) | copy-start | bytes 388
